TPU v7x, 128 devices: a whole 4x4x4 slice. The times are simulated.
128 devices in a mesh: grp: 16 (over z, x), nar: 8 (over y, core).
Axes of the slice: x: 4, y: 4, z: 4, core: 2. Of those that a mesh axis runs over, the one named last changes fastest.
Arguments:
- run_desc: bfloat16 [524288, 256], P(('grp', 'nar')), may hold values from -48 to 48
- ref_desc: bfloat16 [8192, 256], P('nar'), may hold values from -6 to 6
- candidates: int32 [4096, 8], P(('grp', 'nar')), may hold values from 0 to 63, as said below
- live_slots: int32 [4096], P(('grp', 'nar')), may hold values from 1 to 8, as said below
- run_mass: float32 [524288], P(('grp', 'nar')), may hold values from 0.1 to 2
- ref_mass: float32 [8192], P('nar'), may hold values from 0.1 to 2
- ref_start: float32 [8192], P('nar'), may hold values from -62 to 42
Outputs:
- run_potential: float32 [524288], P(('grp', 'nar'))
- ref_potential: float32 [8192], P('nar')
Inputs may be any that keep to these rules, and one draw needn't show every extreme that they name: `candidates`: each row holds 8 different reference block numbers; every reference block is the first entry of some row. `live_slots`: the first run block of each device has all 8 slots live.
All inputs are finite; a program needn't handle non-finite values.
Results may differ from a plain program's by a relative error of at most 0.0003.
Values may be sent and summed in bfloat16 or wider, within the bound.
A program may use at most 128 MiB of HBM per device.

v0:
```python
import math

import jax
import jax.numpy as jnp
from jax import lax
from jax.sharding import Mesh
from jax.sharding import PartitionSpec as P

BLK = 128
TOPC = 8
ITERS = 3
NAR = ("nar_0", "nar_1")
GRP_NAR = ("grp_0", "grp_1", "nar_0", "nar_1")


entropic = 0.5
floor_value = -1e30


def rows_first(arrays, axis, dims):
    turned = [jnp.moveaxis(a, dim, 0) for a, dim in zip(arrays, dims)]
    widths = [t[0].size for t in turned]
    both = jnp.concatenate([t.reshape(-1, w) for t, w in zip(turned, widths)], axis=1)
    result = lax.all_gather(both, axis, axis=0, tiled=True)
    parts = jnp.split(result, [sum(widths[:k]) for k in range(1, len(widths))], axis=1)
    return tuple(
        (
            jnp.moveaxis(b.reshape(-1, *t.shape[1:]), 0, dim)
            for b, t, dim in zip(parts, turned, dims)
        )
    )


def gathered_once(array, axis):
    leaves = jax.tree.leaves(array)
    turns = sorted(range(len(leaves)), key=lambda k: -leaves[k].size)
    width = (1, *leaves[turns[0]].shape)[-1]
    lines = [
        jnp.pad(leaves[k].reshape(-1), (0, -leaves[k].size % width)).reshape(-1, width)
        for k in turns
    ]
    both, at, found = (lax.all_gather(jnp.concatenate(lines), axis), 0, {})
    for k, line in zip(turns, lines):
        share = both[:, at : at + len(line)].reshape(len(both), -1)
        found[k] = share[:, : leaves[k].size].reshape(-1, *leaves[k].shape)
        at += len(line)
    numbers = iter(range(len(leaves)))
    return jax.tree.map(lambda _: found[next(numbers)], array)


def once_a_type(array, axis):
    leaves, found = (jax.tree.leaves(array), {})
    for leading, a in enumerate(leaves):
        if leading not in found:
            alike = [k for k, b in enumerate(leaves) if b.dtype == a.dtype]
            got = (
                gathered_once([leaves[k] for k in alike], axis)
                if len(alike) > 1
                else [lax.all_gather(a, axis)]
            )
            for k, b in zip(alike, got):
                found[k] = b
    numbers = iter(range(len(leaves)))
    return jax.tree.map(lambda _: found[next(numbers)], array)


def combined_by_axis(array, axes, combine):
    for axis in axes:
        pieces = once_a_type(array, axis)
        array = jax.tree.map(lambda part: part[0], pieces)
        for k in range(1, lax.axis_size(axis)):
            array = combine(array, jax.tree.map(lambda part: part[k], pieces))
    return array


def merge_pair(earlier, later):
    joined_peak = jnp.maximum(earlier[0], later[0])
    joined_total = earlier[1] * jnp.exp(earlier[0] - joined_peak) + later[1] * jnp.exp(
        later[0] - joined_peak
    )
    return (joined_peak, joined_total)


def shards(run_desc, ref_desc, candidates, live_slots, run_mass, ref_mass, ref_start):
    run_blocks = candidates.shape[0]
    feature_width = run_desc.shape[1]
    run_tiles = run_desc.reshape(run_blocks, BLK, feature_width)
    ref_all = lax.all_gather(ref_desc, NAR, axis=0, tiled=True)
    mass_all, start_all = rows_first((ref_mass, ref_start), NAR, (0, 0))
    ref_blocks = ref_all.shape[0] // BLK
    ref_tiles = ref_all.reshape(ref_blocks, BLK, feature_width)
    log_ref = jnp.log(mass_all).reshape(ref_blocks, BLK)
    log_run = jnp.log(run_mass).reshape(run_blocks, BLK)
    live_mask = jnp.arange(TOPC, dtype=jnp.int32)[None, :] < live_slots[:, None]
    ref_index = jnp.arange(ref_blocks, dtype=jnp.int32)
    nar_index = lax.axis_index(NAR)
    own_blocks = ref_blocks // lax.axis_size(NAR)

    def slot_cost(slot_index):
        picked = ref_tiles[candidates[:, slot_index]]
        products = jnp.einsum("rid,rjd->rij", run_tiles, picked, preferred_element_type=jnp.float32)
        return -products / math.sqrt(feature_width)

    potential_ref = start_all.reshape(ref_blocks, BLK)
    potential_run = jnp.zeros((run_blocks, BLK), jnp.float32)
    own_ref = jnp.zeros((own_blocks, BLK), jnp.float32)
    for iteration in range(ITERS):
        row_peak = jnp.full((run_blocks, BLK), floor_value, jnp.float32)
        row_total = jnp.zeros((run_blocks, BLK), jnp.float32)
        for row_slot_index in range(TOPC):
            shifted = potential_ref[candidates[:, row_slot_index]]
            row_scores = (shifted[:, None, :] - slot_cost(row_slot_index)) / entropic
            row_slot_peak = jnp.max(row_scores, axis=2)
            row_slot_total = jnp.sum(jnp.exp(row_scores - row_slot_peak[:, :, None]), axis=2)
            row_active = live_mask[:, row_slot_index][:, None]
            row_slot_peak = jnp.where(row_active, row_slot_peak, floor_value)
            row_slot_total = jnp.where(row_active, row_slot_total, 0.0)
            row_peak, row_total = merge_pair((row_peak, row_total), (row_slot_peak, row_slot_total))
        potential_run = entropic * log_run - entropic * (row_peak + jnp.log(row_total))
        slot_peaks = []
        slot_totals = []
        onehots = []
        for column_slot_index in range(TOPC):
            scores = (potential_run[:, :, None] - slot_cost(column_slot_index)) / entropic
            slot_peak = jnp.max(scores, axis=1)
            slot_total = jnp.sum(jnp.exp(scores - slot_peak[:, None, :]), axis=1)
            active = live_mask[:, column_slot_index][:, None]
            slot_peaks.append(jnp.where(active, slot_peak, floor_value))
            slot_totals.append(jnp.where(active, slot_total, 0.0))
            onehots.append(candidates[:, column_slot_index][:, None] == ref_index[None, :])
        dense_peak = jnp.full((ref_blocks, BLK), floor_value, jnp.float32)
        for column_slot_index in range(TOPC):
            spread = jnp.where(
                onehots[column_slot_index][:, :, None],
                slot_peaks[column_slot_index][:, None, :],
                floor_value,
            )
            dense_peak = jnp.maximum(dense_peak, jnp.max(spread, axis=0))
        dense_total = jnp.zeros((ref_blocks, BLK), jnp.float32)
        for column_slot_index in range(TOPC):
            lifted = dense_peak[candidates[:, column_slot_index]]
            scaled = slot_totals[column_slot_index] * jnp.exp(
                slot_peaks[column_slot_index] - lifted
            )
            dense_total = dense_total + jnp.einsum(
                "rb,rj->bj",
                onehots[column_slot_index].astype(jnp.float32),
                scaled,
                precision=lax.Precision.HIGHEST,
            )
        dense_peak, dense_total = (dense_peak, dense_total)
        global_peak, global_total = combined_by_axis((dense_peak, dense_total), GRP_NAR, merge_pair)
        potential_ref = entropic * log_ref - entropic * (global_peak + jnp.log(global_total))
        own_ref = lax.dynamic_slice_in_dim(potential_ref, nar_index * own_blocks, own_blocks, 0)
    return (potential_run.reshape(-1), own_ref.reshape(-1))


def solution(mesh):
    finer = Mesh(mesh.devices.reshape(4, 4, 4, 2), ("grp_0", "grp_1", "nar_0", "nar_1"))
    return jax.shard_map(
        shards,
        mesh=finer,
        in_specs=(
            P(GRP_NAR, None),
            P(NAR, None),
            P(GRP_NAR, None),
            P(GRP_NAR),
            P(GRP_NAR),
            P(NAR),
            P(NAR),
        ),
        out_specs=(P(GRP_NAR), P(NAR)),
        check_vma=False,
    )
```

profile of v0, /device:TPU:1, one launch (start us, length us, event | category | flops | bytes accessed | tf_op | source)
XLA Modules:
  0.0 347.1 jit_solution(5695359694504212478)
XLA Ops:
  8.6 14.6 %all_gather.78 = f32[8192,2]{0,1:T(2,128)S(1)} all-gather(f32[1024,2]{0,1:T(2,128)S(1)} %pad_maximum_fusion.12), channel_id=1, replica_groups=mesh['grp_0'=4,'grp_1'=4,'nar_0'=4,'nar_1'=2] {'nar_0','nar_1'}, dimensions={0}, use_global_device_ids=true | all-gather | bytes 73728 | tf_op jit(solution)/shard_map/all_gather | solution.py:24
  29.9 15.5 %all-gather.14.cloned.1.call-done = bf16[8192,256]{1,0:T(8,128)(2,1)} async-done(((bf16[1024,256]{1,0:T(8,128)(2,1)}), bf16[8192,256]{1,0:T(8,128)(2,1)}) %all-gather.14.cloned.1.call-update) | async-done | bytes 4194320 | tf_op jit(solution)/shard_map/all_gather | solution.py:88
  45.4 4.2 %gather_fusion.13 = bf16[32,128,256]{2,1,0:T(8,128)(2,1)} fusion(bf16[64,128,256]{2,1,0:T(8,128)(2,1)} %bitcast.1354, s32[1024]{0:T(1024)S(1)} %get-tuple-element.123), kind=kCustom, calls=%fused_computation.13 | custom fusion | bytes 4194432 | tf_op jit(solution)/shard_map/gather | solution.py:100
  49.6 4.2 %gather_fusion.11 = bf16[32,128,256]{2,1,0:T(8,128)(2,1)} fusion(bf16[64,128,256]{2,1,0:T(8,128)(2,1)} %bitcast.1355, s32[1024]{0:T(1024)S(1)} %get-tuple-element.124), kind=kCustom, calls=%fused_computation.11 | custom fusion | bytes 4194432 | tf_op jit(solution)/shard_map/gather | solution.py:100
  53.8 4.2 %gather_fusion.9 = bf16[32,128,256]{2,1,0:T(8,128)(2,1)} fusion(bf16[64,128,256]{2,1,0:T(8,128)(2,1)} %bitcast.1356, s32[1024]{0:T(1024)S(1)} %get-tuple-element.125), kind=kCustom, calls=%fused_computation.9 | custom fusion | bytes 4194432 | tf_op jit(solution)/shard_map/gather | solution.py:100
  57.9 4.2 %gather_fusion.7 = bf16[32,128,256]{2,1,0:T(8,128)(2,1)} fusion(bf16[64,128,256]{2,1,0:T(8,128)(2,1)} %bitcast.1357, s32[1024]{0:T(1024)S(1)} %get-tuple-element.126), kind=kCustom, calls=%fused_computation.7 | custom fusion | bytes 4194432 | tf_op jit(solution)/shard_map/gather | solution.py:100
  62.1 4.2 %gather_fusion.5 = bf16[32,128,256]{2,1,0:T(8,128)(2,1)} fusion(bf16[64,128,256]{2,1,0:T(8,128)(2,1)} %bitcast.1358, s32[1024]{0:T(1024)S(1)} %get-tuple-element.127), kind=kCustom, calls=%fused_computation.5 | custom fusion | bytes 4194432 | tf_op jit(solution)/shard_map/gather | solution.py:100
  66.4 4.3 %gather_fusion.3 = bf16[32,128,256]{2,1,0:T(8,128)(2,1)} fusion(bf16[64,128,256]{2,1,0:T(8,128)(2,1)} %bitcast.1359, s32[1024]{0:T(1024)S(1)} %get-tuple-element.128), kind=kCustom, calls=%fused_computation.3 | custom fusion | bytes 4194432 | tf_op jit(solution)/shard_map/gather | solution.py:100
  70.6 4.2 %gather_fusion.1 = bf16[32,128,256]{2,1,0:T(8,128)(2,1)} fusion(bf16[64,128,256]{2,1,0:T(8,128)(2,1)} %bitcast.1360, s32[1024]{0:T(1024)S(1)} %get-tuple-element.129), kind=kCustom, calls=%fused_computation.1 | custom fusion | bytes 4194432 | tf_op jit(solution)/shard_map/gather | solution.py:100
  74.8 4.2 %gather_fusion.15 = bf16[32,128,256]{2,1,0:T(8,128)(2,1)} fusion(bf16[64,128,256]{2,1,0:T(8,128)(2,1)} %bitcast.1361, s32[1024]{0:T(1024)S(1)} %get-tuple-element.122), kind=kCustom, calls=%fused_computation.15 | custom fusion | bytes 4194432 | tf_op jit(solution)/shard_map/gather | solution.py:100
  79.0 2.7 bitcast_reduce_fusion.41
  107.0 5.9 %fusion.65 = (f32[32,128]{1,0:T(8,128)S(1)}, f32[32,128]{1,0:T(8,128)S(1)}, f32[32,128]{1,0:T(8,128)S(1)}, f32[32,128]{1,0:T(8,128)S(1)}, f32[32,128]{1,0:T(8,12...) fusion(f32[32,128,128]{2,1,0:T(8,128)S(1)} %get-tuple-element.99, ...), kind=kLoop, calls=%fused_computation.187 | loop fusion | flops 13598720 | bytes 16957440 | tf_op jit(solution)/shard_map/reduce_sum | solution.py:126
  113.3 7.7 %fusion.67 = (f32[32,128]{1,0:T(8,128)S(1)}, f32[32,128]{1,0:T(8,128)S(1)}, f32[32,128]{1,0:T(8,128)S(1)}, f32[32,128]{1,0:T(8,128)S(1)}, f32[32,128]{1,0:T(8,128)S(1)}, /*index=5*/f32[32,128]{1,0:T(8,128)S(1)}) fusion(f32[32,128,128]{2,1,0:T(8,128)S(1)} %get-tuple-element.101, f32[32,128]{1,0:T(8,128)S(1)} %get-tuple-element.40, ...), kind=kLoop, calls=%fused_computation.191 | loop fusion | flops 12558336 | bytes 12795904 | tf_op jit(solution)/shard_map/reduce_sum | solution.py:126
  131.0 10.4 %all-gather = f32[512,128]{1,0:T(8,128)S(1)} all-gather(f32[128,128]{1,0:T(8,128)S(1)} %pad_maximum_fusion), channel_id=2, replica_groups=mesh['grp_0'=4,'grp_1'=4,'nar_0'=4,'nar_1'=2] {'grp_0'}, dimensions={0}, use_global_device_ids=true | all-gather | bytes 327680 | tf_op jit(solution)/shard_map/all_gather | solution.py:42
  141.5 9.7 %all-gather.1 = f32[512,128]{1,0:T(8,128)S(1)} all-gather(f32[128,128]{1,0:T(8,128)S(1)} %pad_maximum_fusion.1), channel_id=3, replica_groups=mesh['grp_0'=4,'grp_1'=4,'nar_0'=4,'nar_1'=2] {'grp_1'}, dimensions={0}, use_global_device_ids=true | all-gather | bytes 327680 | tf_op jit(solution)/shard_map/all_gather | solution.py:42
  151.2 9.7 %all-gather.2 = f32[512,128]{1,0:T(8,128)S(1)} all-gather(f32[128,128]{1,0:T(8,128)S(1)} %pad_maximum_fusion.2), channel_id=4, replica_groups=mesh['grp_0'=4,'grp_1'=4,'nar_0'=4,'nar_1'=2] {'nar_0'}, dimensions={0}, use_global_device_ids=true | all-gather | bytes 327680 | tf_op jit(solution)/shard_map/all_gather | solution.py:42
  160.9 9.8 %all-gather.3 = f32[256,128]{1,0:T(8,128)S(1)} all-gather(f32[128,128]{1,0:T(8,128)S(1)} %pad_maximum_fusion.3), channel_id=5, replica_groups=mesh['grp_0'=4,'grp_1'=4,'nar_0'=4,'nar_1'=2] {'nar_1'}, dimensions={0}, use_global_device_ids=true | all-gather | bytes 196608 | tf_op jit(solution)/shard_map/all_gather | solution.py:42
  175.4 2.1 bitcast_reduce_fusion.31
  177.5 2.0 fusion.63
  191.8 5.9 %fusion.33 = (f32[32,128]{1,0:T(8,128)S(1)}, f32[32,128]{1,0:T(8,128)S(1)}, f32[32,128]{1,0:T(8,128)S(1)}, f32[32,128]{1,0:T(8,128)S(1)}, f32[32,128]{1,0:T(8,12...) fusion(f32[32,128,128]{2,1,0:T(8,128)S(1)} %copy-done.23, ...), kind=kLoop, calls=%fused_computation.123 | loop fusion | flops 13598720 | bytes 16957440 | tf_op jit(solution)/shard_map/reduce_sum | solution.py:126
  198.1 7.7 %fusion.35 = (f32[32,128]{1,0:T(8,128)S(1)}, f32[32,128]{1,0:T(8,128)S(1)}, f32[32,128]{1,0:T(8,128)S(1)}, f32[32,128]{1,0:T(8,128)S(1)}, f32[32,128]{1,0:T(8,128)S(1)}, /*index=5*/f32[32,128]{1,0:T(8,128)S(1)}) fusion(f32[32,128,128]{2,1,0:T(8,128)S(1)} %copy-done.2, f32[32,128]{1,0:T(8,128)S(1)} %get-tuple-element.24, ...), kind=kLoop, calls=%fused_computation.127 | loop fusion | flops 12558336 | bytes 12795904 | tf_op jit(solution)/shard_map/reduce_sum | solution.py:126
  215.8 9.8 %all-gather.4 = f32[512,128]{1,0:T(8,128)S(1)} all-gather(f32[128,128]{1,0:T(8,128)S(1)} %pad_maximum_fusion.4), channel_id=6, replica_groups=mesh['grp_0'=4,'grp_1'=4,'nar_0'=4,'nar_1'=2] {'grp_0'}, dimensions={0}, use_global_device_ids=true | all-gather | bytes 327680 | tf_op jit(solution)/shard_map/all_gather | solution.py:42
  225.6 9.4 %all-gather.5 = f32[512,128]{1,0:T(8,128)S(1)} all-gather(f32[128,128]{1,0:T(8,128)S(1)} %pad_maximum_fusion.5), channel_id=7, replica_groups=mesh['grp_0'=4,'grp_1'=4,'nar_0'=4,'nar_1'=2] {'grp_1'}, dimensions={0}, use_global_device_ids=true | all-gather | bytes 327680 | tf_op jit(solution)/shard_map/all_gather | solution.py:42
  235.1 9.4 %all-gather.6 = f32[512,128]{1,0:T(8,128)S(1)} all-gather(f32[128,128]{1,0:T(8,128)S(1)} %pad_maximum_fusion.6), channel_id=8, replica_groups=mesh['grp_0'=4,'grp_1'=4,'nar_0'=4,'nar_1'=2] {'nar_0'}, dimensions={0}, use_global_device_ids=true | all-gather | bytes 327680 | tf_op jit(solution)/shard_map/all_gather | solution.py:42
  244.5 10.2 %all-gather.7 = f32[256,128]{1,0:T(8,128)S(1)} all-gather(f32[128,128]{1,0:T(8,128)S(1)} %pad_maximum_fusion.7), channel_id=9, replica_groups=mesh['grp_0'=4,'grp_1'=4,'nar_0'=4,'nar_1'=2] {'nar_1'}, dimensions={0}, use_global_device_ids=true | all-gather | bytes 196608 | tf_op jit(solution)/shard_map/all_gather | solution.py:42
  259.3 2.1 bitcast_reduce_fusion.15
  275.7 5.9 %fusion.1 = (f32[32,128]{1,0:T(8,128)S(1)}, f32[32,128]{1,0:T(8,128)S(1)}, f32[32,128]{1,0:T(8,128)S(1)}, f32[32,128]{1,0:T(8,128)S(1)}, f32[32,128]{1,0:T(8,128...) fusion(f32[32,128,128]{2,1,0:T(8,128)S(1)} %copy-done.24, ...), kind=kLoop, calls=%fused_computation.59 | loop fusion | flops 13598720 | bytes 16957440 | tf_op jit(solution)/shard_map/reduce_sum | solution.py:126
  281.9 7.8 %fusion.3 = (f32[32,128]{1,0:T(8,128)S(1)}, f32[32,128]{1,0:T(8,128)S(1)}, f32[32,128]{1,0:T(8,128)S(1)}, f32[32,128]{1,0:T(8,128)S(1)}, f32[32,128]{1,0:T(8,128)S(1)}, /*index=5*/f32[32,128]{1,0:T(8,128)S(1)}) fusion(f32[32,128,128]{2,1,0:T(8,128)S(1)} %copy-done.3, f32[32,128]{1,0:T(8,128)S(1)} %get-tuple-element.8, ...), kind=kLoop, calls=%fused_computation.63 | loop fusion | flops 12558336 | bytes 12795904 | tf_op jit(solution)/shard_map/reduce_sum | solution.py:126
  299.7 9.7 %all-gather.8 = f32[512,128]{1,0:T(8,128)S(1)} all-gather(f32[128,128]{1,0:T(8,128)S(1)} %pad_maximum_fusion.8), channel_id=10, replica_groups=mesh['grp_0'=4,'grp_1'=4,'nar_0'=4,'nar_1'=2] {'grp_0'}, dimensions={0}, use_global_device_ids=true | all-gather | bytes 327680 | tf_op jit(solution)/shard_map/all_gather | solution.py:42
  309.5 9.4 %all-gather.9 = f32[512,128]{1,0:T(8,128)S(1)} all-gather(f32[128,128]{1,0:T(8,128)S(1)} %pad_maximum_fusion.9), channel_id=11, replica_groups=mesh['grp_0'=4,'grp_1'=4,'nar_0'=4,'nar_1'=2] {'grp_1'}, dimensions={0}, use_global_device_ids=true | all-gather | bytes 327680 | tf_op jit(solution)/shard_map/all_gather | solution.py:42
  318.9 9.4 %all-gather.10 = f32[512,128]{1,0:T(8,128)S(1)} all-gather(f32[128,128]{1,0:T(8,128)S(1)} %pad_maximum_fusion.10), channel_id=12, replica_groups=mesh['grp_0'=4,'grp_1'=4,'nar_0'=4,'nar_1'=2] {'nar_0'}, dimensions={0}, use_global_device_ids=true | all-gather | bytes 327680 | tf_op jit(solution)/shard_map/all_gather | solution.py:42
  328.3 10.3 %all-gather.11 = f32[256,128]{1,0:T(8,128)S(1)} all-gather(f32[128,128]{1,0:T(8,128)S(1)} %pad_maximum_fusion.11), channel_id=13, replica_groups=mesh['grp_0'=4,'grp_1'=4,'nar_0'=4,'nar_1'=2] {'nar_1'}, dimensions={0}, use_global_device_ids=true | all-gather | bytes 196608 | tf_op jit(solution)/shard_map/all_gather | solution.py:42
  (282 shorter events, 101.1 us)
Async XLA Ops:
  7.2 71.9 %copy-start = (bf16[4096,256]{1,0:T(8,128)(2,1)S(1)}, bf16[4096,256]{1,0:T(8,128)(2,1)}, u32[]{:S(2)}) copy-start(bf16[4096,256]{1,0:T(8,128)(2,1)} %param.7) | copy-start | bytes 6291460
  7.2 38.2 %all-gather.14.cloned.1.call-start = ((), (), s32[]{:S(2)}) async-start(), calls=%async_computation | async-start | bytes 4718592 | tf_op jit(solution)/shard_map/all_gather | solution.py:88
  81.7 31.5 %copy-start.1 = (f32[32,128,128]{2,1,0:T(8,128)}, f32[32,128,128]{2,1,0:T(8,128)S(1)}, u32[]{:S(2)}) copy-start(f32[32,128,128]{2,1,0:T(8,128)S(1)} %get-tuple-element.101) | copy-start | bytes 6291460
  81.7 2.3 copy-start.31
  85.0 28.2 %copy-start.4 = (f32[32,128,128]{2,1,0:T(8,128)}, f32[32,128,128]{2,1,0:T(8,128)S(1)}, u32[]{:S(2)}) copy-start(f32[32,128,128]{2,1,0:T(8,128)S(1)} %get-tuple-element.103) | copy-start | bytes 6291460
  85.1 2.3 copy-start.30
  88.3 24.9 %copy-start.7 = (f32[32,128,128]{2,1,0:T(8,128)}, f32[32,128,128]{2,1,0:T(8,128)S(1)}, u32[]{:S(2)}) copy-start(f32[32,128,128]{2,1,0:T(8,128)S(1)} %get-tuple-element.105) | copy-start | bytes 6291460
  88.4 2.3 copy-start.29
  91.7 21.6 %copy-start.10 = (f32[32,128,128]{2,1,0:T(8,128)}, f32[32,128,128]{2,1,0:T(8,128)S(1)}, u32[]{:S(2)}) copy-start(f32[32,128,128]{2,1,0:T(8,128)S(1)} %get-tuple-element.107) | copy-start | bytes 6291460
  91.7 2.3 copy-start.28
  95.0 18.3 %copy-start.13 = (f32[32,128,128]{2,1,0:T(8,128)}, f32[32,128,128]{2,1,0:T(8,128)S(1)}, u32[]{:S(2)}) copy-start(f32[32,128,128]{2,1,0:T(8,128)S(1)} %get-tuple-element.109) | copy-start | bytes 6291460
  95.0 2.3 copy-start.27
  98.3 15.0 %copy-start.16 = (f32[32,128,128]{2,1,0:T(8,128)}, f32[32,128,128]{2,1,0:T(8,128)S(1)}, u32[]{:S(2)}) copy-start(f32[32,128,128]{2,1,0:T(8,128)S(1)} %get-tuple-element.111) | copy-start | bytes 6291460
  98.3 2.3 copy-start.26
  101.6 5.4 %copy-start.19 = (f32[32,128,128]{2,1,0:T(8,128)}, f32[32,128,128]{2,1,0:T(8,128)S(1)}, u32[]{:S(2)}) copy-start(f32[32,128,128]{2,1,0:T(8,128)S(1)} %get-tuple-element.113) | copy-start | bytes 6291460
  101.6 2.3 copy-start.25
  104.9 2.1 copy-start.22
  175.4 4.1 %copy-start.17 = (f32[32,128,128]{2,1,0:T(8,128)S(1)}, f32[32,128,128]{2,1,0:T(8,128)}, u32[]{:S(2)}) copy-start(f32[32,128,128]{2,1,0:T(8,128)} %copy-done.16) | copy-start | bytes 6291460
  179.5 1.6 copy-start.14
  181.1 1.6 copy-start.11
  182.7 1.6 copy-start.8
  184.2 1.6 copy-start.5
  185.8 1.6 copy-start.2
  187.4 1.6 copy-start.23
  189.0 1.6 copy-start.20
  259.3 4.1 %copy-start.18 = (f32[32,128,128]{2,1,0:T(8,128)S(1)}, f32[32,128,128]{2,1,0:T(8,128)}, u32[]{:S(2)}) copy-start(f32[32,128,128]{2,1,0:T(8,128)} %copy-done.16) | copy-start | bytes 6291460
  263.4 1.6 copy-start.15
  265.0 1.6 copy-start.12
  266.6 1.6 copy-start.9
  268.1 1.6 copy-start.6
  269.7 1.6 copy-start.3
  272.9 1.6 copy-start.21
  (2 other events, 2.3 us)
Sparse Core Ops, SparseCore 0:
  9.7 35.6 all-gather.13
where the time goes:
time: 351 us; the launch traced here: 347 us
  blocking collectives  132 us (38%)
  other arithmetic  93.4 us (27%)
  local copies, waits for them, and re-layouts  74 us (21%)
  matrix products  16.2 us (5%)
  waiting for transfers between devices  16.1 us (5%)
  between operations  15.7 us (4%)
    all_gather x12, blocking collectives, gathered_once(): both, at, found = (lax.all_gather(jnp.concatenate(lines), axis), 0, {})  117 us
    reduce_sum x6, other arithmetic, shards(): slot_total = jnp.sum(jnp.exp(scores - slot_peak[:, None, :]), axis=1)  40.9 us
    gather x8, local copies, waits for them, and re-layouts, slot_cost(): picked = ref_tiles[candidates[:, slot_index]]  33.6 us
    reduce_sum x24, other arithmetic, shards(): jnp.sum(jnp.exp(row_scores - row_slot_peak[:, :, None]), axis=2)  20.1 us
    all_gather x1, waiting for transfers between devices, shards(): ref_all = lax.all_gather(ref_desc, NAR, axis=0, tiled=True)  15.5 us
    all_gather x1, blocking collectives, rows_first(): result = lax.all_gather(both, axis, axis=0, tiled=True)  14.6 us
    reduce_max x16, other arithmetic, shards(): row_slot_peak = jnp.max(row_scores, axis=2)  14 us
    gather x24, local copies, waits for them, and re-layouts, shards(): shifted = potential_ref[candidates[:, row_slot_index]]  13.8 us
  transfers between devices with their start and end apart: 1, of which 1 were waited for; matrix products, arithmetic and copies ran while one was open for 2% of the time, Pallas kernels for 0%

commit v1 on v0

v1 whole, which is shorter than its diff:
```python
import math

import jax
import jax.numpy as jnp
from jax import lax
from jax.experimental import pallas as pl
from jax.experimental.pallas import tpu as pltpu
from jax.sharding import PartitionSpec as P

BLK = 128
TOPC = 8
RB = 32
ENT = RB * TOPC
D = 256
REFB = 64
NAR = 8
GRP = 16
LOG2E = math.log2(math.e)
LN2 = math.log(2.0)
FLOOR = -1e30
MESH = pl.DeviceIdType.MESH
F32 = jnp.float32
BF16 = jnp.bfloat16


def kernel(
    cand,
    live,
    run_hbm,
    ref_hbm,
    run_mass,
    ref_mass,
    start,
    out_run,
    out_ref,
    ref_all,
    run_v,
    tiles,
    v_all,
    rows_a,
    rows_m,
    rows_t,
    rows_live,
    onehot_t,
    onehot,
    a_col,
    loga_col,
    r_col,
    u_col,
    dense,
    peak,
    rs_buf,
    part,
    ar_buf,
    final,
    ag_buf,
    local_sem,
    own_send,
    gather_send,
    gather_recv,
    pair_send,
    pair_recv,
    start_send,
    start_recv,
    rs_send,
    rs_recv,
    ar_send,
    ar_recv,
    ag_send,
    ag_recv,
):
    g = lax.axis_index("grp")
    n = lax.axis_index("nar")
    z, x = lax.div(g, 4), lax.rem(g, 4)
    y, c = lax.div(n, 2), lax.rem(n, 2)

    barrier = pltpu.get_barrier_semaphore()
    for k in range(1, NAR):
        pl.semaphore_signal(
            barrier, inc=1, device_id=(g, lax.rem(n + k, NAR)), device_id_type=MESH
        )
    for k in range(1, GRP):
        pl.semaphore_signal(
            barrier, inc=1, device_id=(lax.rem(g + k, GRP), n), device_id_type=MESH
        )

    own_copy = pltpu.make_async_copy(ref_hbm, ref_all.at[pl.ds(n * 8, 8)], local_sem.at[0])
    own_copy.start()
    run_copy = pltpu.make_async_copy(run_hbm, run_v, local_sem.at[1])
    run_copy.start()

    pl.semaphore_wait(barrier, NAR + GRP - 2)

    partner = (g, y * 2 + 1 - c)
    y_next = (g, lax.rem(y + 1, 4) * 2 + c)
    y_prev = (g, lax.rem(y + 3, 4) * 2 + c)
    x_next = (z * 4 + lax.rem(x + 1, 4), n)
    x_prev = (z * 4 + lax.rem(x + 3, 4), n)
    z_next = (lax.rem(z + 1, 4) * 4 + x, n)
    z_prev = (lax.rem(z + 3, 4) * 4 + x, n)
    s_prev = y_prev[1]
    s_next = y_next[1]
    s_far = lax.rem(y + 2, 4) * 2 + c

    sent = []

    def send(src, dst, send_sem, recv_sem, to):
        copy = pltpu.make_async_remote_copy(
            src_ref=src,
            dst_ref=dst,
            send_sem=send_sem,
            recv_sem=recv_sem,
            device_id=to,
            device_id_type=MESH,
        )
        copy.start()
        sent.append(copy)

    def arrived(dst, recv_sem):
        pltpu.make_async_remote_copy(
            src_ref=dst,
            dst_ref=dst,
            send_sem=own_send.at[0],
            recv_sem=recv_sem,
            device_id=partner,
            device_id_type=MESH,
        ).wait_recv()

    counter = [0]

    def region(block, half):
        if half is None:
            return ref_all.at[block]
        return ref_all.at[block, pl.ds(half * 64, 64)]

    def gsend(block, half, ident, to, src=None):
        dst = region(block, half)
        k = counter[0]
        counter[0] += 1
        send(dst if src is None else src, dst, gather_send.at[k], gather_recv.at[ident], to)

    def to_partner(block, half, ident):
        dst = region(block, half)
        send(dst, dst, pair_send.at[ident], pair_recv.at[ident], partner)

    own_a, own_b = n * 8 + x, n * 8 + 4 + z
    gsend(own_a, None, 0, y_next, ref_hbm.at[x])
    gsend(own_a, None, 1, y_prev, ref_hbm.at[x])
    gsend(own_b, None, 2, y_next, ref_hbm.at[4 + z])
    gsend(own_b, None, 3, y_prev, ref_hbm.at[4 + z])
    for k in range(1, NAR):
        send(
            start,
            v_all.at[pl.ds(n * 8, 8)],
            start_send.at[k],
            start_recv.at[k],
            (g, lax.rem(n + k, NAR)),
        )
    send(ref_hbm, ref_all.at[pl.ds(n * 8, 8)], pair_send.at[30], pair_recv.at[30], partner)
    v_all[pl.ds(n * 8, 8)] = start[...]

    lane64 = lax.broadcasted_iota(jnp.int32, (1, BLK), 1)

    def table_step(b, carry):
        for t in range(TOPC):
            e = b * TOPC + t
            onehot_t[pl.ds(e, 1)] = jnp.where(lane64 == cand[b, t], 1.0, 0.0).astype(F32)
            rows_live[pl.ds(e, 1)] = jnp.where(
                jnp.full((1, BLK), t, jnp.int32) < live[b], 1.0, 0.0
            ).astype(F32)
        return carry

    lax.fori_loop(0, RB, table_step, 0)

    a_prev, a_next, a_far = s_prev * 8 + x, s_next * 8 + x, s_far * 8 + x
    b_prev, b_next, b_far = s_prev * 8 + 4 + z, s_next * 8 + 4 + z, s_far * 8 + 4 + z

    def y_piece(block, ident, j, along_x, far_to, far_ident):
        arrived(region(block, None), gather_recv.at[ident])
        if far_to is not None:
            gsend(block, None, far_ident, far_to)
        base = 6 if along_x else 18
        up, down = (x_next, x_prev) if along_x else (z_next, z_prev)
        gsend(block, None, base + j, up)
        gsend(block, None, base + 3 + j, down)
        to_partner(block, None, ident)

    y_piece(a_prev, 0, 0, True, y_next, 4)
    y_piece(b_next, 3, 1, False, y_prev, 5)
    y_piece(a_next, 1, 1, True, None, None)
    y_piece(b_prev, 2, 0, False, None, None)
    y_piece(a_far, 4, 2, True, None, None)
    y_piece(b_far, 5, 2, False, None, None)

    shard = (s_prev, s_next, s_far)
    x_up, x_down, x_far = lax.rem(x + 3, 4), lax.rem(x + 1, 4), lax.rem(x + 2, 4)
    z_up, z_down, z_far = lax.rem(z + 3, 4), lax.rem(z + 1, 4), lax.rem(z + 2, 4)

    def ring_piece(j, along_x):
        base = 6 if along_x else 18
        off = 0 if along_x else 4
        from_prev = shard[j] * 8 + off + (x_up if along_x else z_up)
        from_next = shard[j] * 8 + off + (x_down if along_x else z_down)
        up, down = (x_next, x_prev) if along_x else (z_next, z_prev)
        arrived(region(from_prev, None), gather_recv.at[base + j])
        gsend(from_prev, 0, base + 6 + j, up)
        to_partner(from_prev, None, base + j)
        arrived(region(from_next, None), gather_recv.at[base + 3 + j])
        gsend(from_next, 1, base + 9 + j, down)
        to_partner(from_next, None, base + 3 + j)

    def far_piece(j, along_x):
        base = 6 if along_x else 18
        off = 0 if along_x else 4
        block = shard[j] * 8 + off + (x_far if along_x else z_far)
        for half in range(2):
            ident = base + 6 + 3 * half + j
            arrived(region(block, half), gather_recv.at[ident])
            to_partner(block, half, ident)

    ring_piece(0, True)
    ring_piece(1, False)
    ring_piece(1, True)
    ring_piece(0, False)
    ring_piece(2, True)
    ring_piece(2, False)

    eye = lax.broadcasted_iota(jnp.int32, (BLK, BLK), 0) == lax.broadcasted_iota(
        jnp.int32, (BLK, BLK), 1
    )
    wide = (BLK, BLK)

    def column(row):
        spread = jnp.where(eye, jnp.broadcast_to(row, wide), 0.0)
        return jnp.broadcast_to(jnp.sum(spread, axis=1, keepdims=True), wide)

    def mass_step(b, carry):
        row = run_mass[pl.ds(b, 1)]
        a_col[b] = column(row)
        loga_col[b] = column(jnp.log(row) * LOG2E)
        return carry

    lax.fori_loop(0, RB, mass_step, 0)
    onehot[...] = onehot_t[...].T.astype(BF16)

    for k in range(1, NAR):
        owner = lax.rem(n + NAR - k, NAR)
        arrived(v_all.at[pl.ds(owner * 8, 8)], start_recv.at[k])

    def pick_rows(table, to):
        def step(b, carry):
            for t in range(TOPC):
                to[pl.ds(b * TOPC + t, 1)] = table[pl.ds(cand[b, t], 1)]
            return carry

        lax.fori_loop(0, RB, step, 0)

    pick_rows(v_all, rows_a)
    alive = rows_live[...] > 0.5
    rows_a[...] = jnp.where(alive, rows_a[...] * (2.0 * LOG2E), FLOOR)

    far_piece(0, True)
    far_piece(1, False)
    far_piece(1, True)
    far_piece(0, False)
    far_piece(2, True)
    far_piece(2, False)

    other = partner[1]
    arrived(ref_all.at[pl.ds(other * 8, 8)], pair_recv.at[30])
    o_shard = tuple(s + 1 - 2 * c for s in shard)
    for j in range(3):
        pass
    pieces = []
    pieces += [(o_shard[0] * 8 + x, None, 0), (o_shard[1] * 8 + x, None, 1)]
    pieces += [(o_shard[0] * 8 + 4 + z, None, 2), (o_shard[1] * 8 + 4 + z, None, 3)]
    pieces += [(o_shard[2] * 8 + x, None, 4), (o_shard[2] * 8 + 4 + z, None, 5)]
    for j in range(3):
        for base, off, up, down, far in (
            (6, 0, x_up, x_down, x_far),
            (18, 4, z_up, z_down, z_far),
        ):
            pieces.append((o_shard[j] * 8 + off + up, None, base + j))
            pieces.append((o_shard[j] * 8 + off + down, None, base + 3 + j))
            pieces.append((o_shard[j] * 8 + off + far, 0, base + 6 + j))
            pieces.append((o_shard[j] * 8 + off + far, 1, base + 9 + j))
    for block, half, ident in pieces:
        arrived(region(block, half), pair_recv.at[ident])
    own_copy.wait()
    run_copy.wait()

    def cost_step(b, carry):
        run = run_v[b]
        top = None
        for h in range(TOPC // 2):
            e = b * TOPC + 2 * h
            both = jnp.concatenate([ref_all[cand[b, 2 * h]], ref_all[cand[b, 2 * h + 1]]], axis=0)
            prod = lax.dot_general(
                run, both, (((1,), (1,)), ((), ())), preferred_element_type=F32
            ) * (LOG2E / 8.0)
            for q in range(2):
                s = prod[:, q * BLK : (q + 1) * BLK]
                tiles[e + q] = s
                s = s + rows_a[pl.ds(e + q, 1)]
                top = s if top is None else jnp.maximum(top, s)
        r_col[b] = jnp.broadcast_to(jnp.max(top, axis=1, keepdims=True), wide)
        return carry

    lax.fori_loop(0, RB, cost_step, 0, unroll=2)

    def row_step(b, carry):
        top = r_col[b]
        total = None
        for t in range(TOPC):
            e = b * TOPC + t
            p = jnp.exp2(tiles[e] + rows_a[pl.ds(e, 1)] - top)
            total = p if total is None else total + p
        total = jnp.broadcast_to(jnp.sum(total, axis=1, keepdims=True), wide)
        u_col[b] = loga_col[b] - (top + jnp.log(total) * LOG2E)
        return carry

    lax.fori_loop(0, RB, row_step, 0, unroll=2)

    def column_step(b, carry):
        u = u_col[b]
        for t in range(TOPC):
            e = b * TOPC + t
            s = tiles[e] + u
            m = jnp.max(s, axis=0, keepdims=True)
            p = jnp.exp2(s - m)
            tiles[e] = p
            rows_m[pl.ds(e, 1)] = m
            rows_t[pl.ds(e, 1)] = jnp.sum(p, axis=0, keepdims=True)
        return carry

    lax.fori_loop(0, RB, column_step, 0, unroll=2)
    alive = rows_live[...] > 0.5
    rows_m[...] = jnp.where(alive, rows_m[...], FLOOR)
    block_id = lax.broadcasted_iota(jnp.int32, (REFB, BLK), 0)

    def peak_step(b, top):
        for t in range(TOPC):
            e = b * TOPC + t
            top = jnp.maximum(
                top, jnp.where(block_id == cand[b, t], rows_m[pl.ds(e, 1)], FLOOR)
            )
        return top

    top = lax.fori_loop(0, RB, peak_step, jnp.full((REFB, BLK), FLOOR, F32))
    peak[...] = top
    pick_rows(peak, rows_a)

    def spread(rows):
        hi = rows.astype(BF16)
        rest = rows - hi.astype(F32)
        mid = rest.astype(BF16)
        low = (rest - mid.astype(F32)).astype(BF16)
        total = None
        for piece in (hi, mid, low):
            d = lax.dot_general(
                onehot[0:REFB], piece, (((1,), (0,)), ((), ())), preferred_element_type=F32
            )
            total = d if total is None else total + d
        return total

    scaled = jnp.where(alive, rows_t[...] * jnp.exp2(rows_m[...] - rows_a[...]), 0.0)
    total = spread(scaled)
    joined = jnp.where(total > 0.0, peak[...] + jnp.log(total) * LOG2E, FLOOR)

    def log_sum(parts):
        top = parts[0]
        for p in parts[1:]:
            top = jnp.maximum(top, p)
        total = None
        for p in parts:
            e = jnp.exp2(p - top)
            total = e if total is None else total + e
        return top + jnp.log(total) * LOG2E

    def plain_sum(parts):
        total = parts[0]
        for p in parts[1:]:
            total = total + p
        return total

    def reduced(it, value, join):
        dense[it] = value
        for k in range(1, NAR):
            to = lax.rem(n + k, NAR)
            send(
                dense.at[it, pl.ds(to * 8, 8)],
                rs_buf.at[it, n],
                rs_send.at[it, k],
                rs_recv.at[it, k],
                (g, to),
            )
        rs_buf[it, n] = dense[it, pl.ds(n * 8, 8)]
        for k in range(1, NAR):
            arrived(rs_buf.at[it, lax.rem(n + NAR - k, NAR)], rs_recv.at[it, k])
        mine = join([rs_buf[it, k] for k in range(NAR)])
        part[it] = mine
        for k in range(1, GRP):
            send(
                part.at[it],
                ar_buf.at[it, g],
                ar_send.at[it, k],
                ar_recv.at[it, k],
                (lax.rem(g + k, GRP), n),
            )
        ar_buf[it, g] = mine
        for k in range(1, GRP):
            arrived(ar_buf.at[it, lax.rem(g + GRP - k, GRP)], ar_recv.at[it, k])
        return join([ar_buf[it, k] for k in range(GRP)])

    def gathered(it, value):
        final[it] = value
        for k in range(1, NAR):
            send(
                final.at[it],
                ag_buf.at[it, pl.ds(n * 8, 8)],
                ag_send.at[it, k],
                ag_recv.at[it, k],
                (g, lax.rem(n + k, NAR)),
            )
        ag_buf[it, pl.ds(n * 8, 8)] = value
        for k in range(1, NAR):
            owner = lax.rem(n + NAR - k, NAR)
            arrived(ag_buf.at[it, pl.ds(owner * 8, 8)], ag_recv.at[it, k])

    column_total = reduced(0, joined, log_sum)
    v_one = jnp.log(ref_mass[...]) * LOG2E - column_total
    gathered(0, v_one)
    pick_rows(ag_buf.at[0], rows_a)
    rows_m[...] = jnp.where(alive, jnp.exp2(rows_m[...] + rows_a[...]), 0.0)
    rows_t[...] = rows_m[...]

    def row_sums(b):
        total = None
        for t in range(TOPC):
            e = b * TOPC + t
            p = tiles[e] * rows_t[pl.ds(e, 1)]
            total = p if total is None else total + p
        return jnp.broadcast_to(jnp.sum(total, axis=1, keepdims=True), wide)

    def second_rows(b, carry):
        r_col[b] = a_col[b] / row_sums(b)
        return carry

    def third_rows(b, carry):
        alpha = a_col[b] / row_sums(b)
        r_col[b] = alpha
        u = (u_col[b] + jnp.log(alpha) * LOG2E) * (0.5 * LN2)
        out_run[pl.ds(b, 1)] = jnp.sum(jnp.where(eye, u, 0.0), axis=0, keepdims=True)
        return carry

    def columns(b, carry):
        alpha = r_col[b]
        for t in range(TOPC):
            e = b * TOPC + t
            rows_a[pl.ds(e, 1)] = jnp.sum(tiles[e] * alpha, axis=0, keepdims=True)
        return carry

    lax.fori_loop(0, RB, second_rows, 0, unroll=2)
    lax.fori_loop(0, RB, columns, 0, unroll=2)
    second = reduced(1, spread(rows_a[...] * rows_m[...]), plain_sum)
    gathered(1, ref_mass[...] / second)
    pick_rows(ag_buf.at[1], rows_a)
    rows_t[...] = rows_m[...] * rows_a[...]
    lax.fori_loop(0, RB, third_rows, 0, unroll=2)
    lax.fori_loop(0, RB, columns, 0, unroll=2)
    third = reduced(2, spread(rows_a[...] * rows_m[...]), plain_sum)
    out_ref[...] = (v_one + jnp.log(ref_mass[...] / third) * LOG2E) * (0.5 * LN2)

    for copy in sent:
        copy.wait_send()


def shards(run_desc, ref_desc, candidates, live_slots, run_mass, ref_mass, ref_start):
    vmem = pl.BlockSpec(memory_space=pltpu.VMEM)
    smem = pl.BlockSpec(memory_space=pltpu.SMEM)
    hbm = pl.BlockSpec(memory_space=pl.ANY)
    dma = pltpu.SemaphoreType.DMA
    run_potential, ref_potential = pl.pallas_call(
        kernel,
        out_shape=(
            jax.ShapeDtypeStruct((RB, BLK), F32),
            jax.ShapeDtypeStruct((8, BLK), F32),
        ),
        in_specs=[smem, smem, hbm, hbm, vmem, vmem, vmem],
        out_specs=(vmem, vmem),
        scratch_shapes=[
            pltpu.VMEM((REFB, BLK, D), BF16),
            pltpu.VMEM((RB, BLK, D), BF16),
            pltpu.VMEM((ENT, BLK, BLK), F32),
            pltpu.VMEM((REFB, BLK), F32),
            pltpu.VMEM((ENT, BLK), F32),
            pltpu.VMEM((ENT, BLK), F32),
            pltpu.VMEM((ENT, BLK), F32),
            pltpu.VMEM((ENT, BLK), F32),
            pltpu.VMEM((ENT, BLK), F32),
            pltpu.VMEM((BLK, ENT), BF16),
            pltpu.VMEM((RB, BLK, BLK), F32),
            pltpu.VMEM((RB, BLK, BLK), F32),
            pltpu.VMEM((RB, BLK, BLK), F32),
            pltpu.VMEM((RB, BLK, BLK), F32),
            pltpu.VMEM((3, REFB, BLK), F32),
            pltpu.VMEM((REFB, BLK), F32),
            pltpu.VMEM((3, NAR, 8, BLK), F32),
            pltpu.VMEM((3, 8, BLK), F32),
            pltpu.VMEM((3, GRP, 8, BLK), F32),
            pltpu.VMEM((2, 8, BLK), F32),
            pltpu.VMEM((2, REFB, BLK), F32),
            dma((2,)),
            dma((1,)),
            dma((32,)),
            dma((30,)),
            dma((31,)),
            dma((31,)),
            dma((NAR,)),
            dma((NAR,)),
            dma((3, NAR)),
            dma((3, NAR)),
            dma((3, GRP)),
            dma((3, GRP)),
            dma((2, NAR)),
            dma((2, NAR)),
        ],
        compiler_params=pltpu.CompilerParams(
            collective_id=0, has_side_effects=True, vmem_limit_bytes=56 * 1024 * 1024
        ),
        name="sinkhorn",
    )(
        candidates,
        live_slots,
        run_desc.reshape(RB, BLK, D),
        ref_desc.reshape(8, BLK, D),
        run_mass.reshape(RB, BLK),
        ref_mass.reshape(8, BLK),
        ref_start.reshape(8, BLK),
    )
    return run_potential.reshape(-1), ref_potential.reshape(-1)


def solution(mesh):
    both = P(("grp", "nar"))
    wide = P(("grp", "nar"), None)
    return jax.shard_map(
        shards,
        mesh=mesh,
        in_specs=(wide, P("nar", None), wide, both, both, P("nar"), P("nar")),
        out_specs=(both, P("nar")),
        check_vma=False,
    )
```

time: 351 us -> 94.1 us (0.27); the launches traced: 347 us -> 93.8 us
  blocking collectives: 132 us -> 0 us
  other arithmetic: 93.4 us -> 0 us
  Pallas kernels: 0 us -> 89.2 us
  local copies, waits for them, and re-layouts: 74 us -> 3.95 us
  matrix products: 16.2 us -> 0 us
  waiting for transfers between devices: 16.1 us -> 0 us
  between operations: 15.7 us -> 0.64 us
    all_gather x13 -> x0, blocking collectives: 132 us -> none  [the longest x12 117 us: gathered_once(): both, at, found = (lax.all_gather(jnp.concatenate(lines), axis), 0, {})]
    pallas_call x0 -> x1, Pallas kernels: none -> 89.2 us  [shards(): pl.pallas_call(kernel, out_shape=(jax.ShapeDtypeStruct((RB, BLK), F32), j...]
    gather x56 -> x0, local copies, waits for them, and re-layouts: 61.1 us -> none  [the longest x8 33.6 us: slot_cost(): picked = ref_tiles[candidates[:, slot_index]]]
    reduce_sum x30 -> x0, other arithmetic: 61 us -> none  [the longest x6 40.9 us: shards(): slot_total = jnp.sum(jnp.exp(scores - slot_peak[:, None, :]), axis=1)]
    reduce_max x43 -> x0, other arithmetic: 25.5 us -> none  [the longest x16 14 us: shards(): row_slot_peak = jnp.max(row_scores, axis=2)]
    dot_general x32 -> x0, matrix products: 16.2 us -> none  [the longest x8 9.27 us: slot_cost(): jnp.einsum('rid,rjd->rij', run_tiles, picked, preferred_element_type=jnp....]
    all_gather x1 -> x0, waiting for transfers between devices: 15.5 us -> none  [shards(): ref_all = lax.all_gather(ref_desc, NAR, axis=0, tiled=True)]
    unnamed x66 -> x3, local copies, waits for them, and re-layouts: 12.9 us -> 3.95 us
  transfers between devices with their start and end apart: 1 -> 0, of which waited for: 1 -> 0; matrix products, arithmetic and copies ran while one was open for 2% -> 0% of each run, Pallas kernels for 0% -> 0%
where the time goes in v1:
time: 94.1 us; the launch traced here: 93.8 us
  Pallas kernels  89.2 us (95%)
  local copies, waits for them, and re-layouts  3.95 us (4%)
    pallas_call x1, Pallas kernels, shards(): pl.pallas_call(kernel, out_shape=(jax.ShapeDtypeStruct((RB, BLK), F32), j...  89.2 us
    unnamed x3, local copies, waits for them, and re-layouts  3.95 us

profile of v1, /device:TPU:1, one launch (start us, length us, event | category | flops | bytes accessed | tf_op | source)
XLA Modules:
  0.0 93.8 jit_solution(15614440156012853344)
XLA Ops:
  0.6 1.4 %copy.9.cand = s32[32,8]{1,0:T(8,128)} copy(s32[32,8]{0,1:T(8,128)} %param.9) | data formatting | bytes 2048 | tf_op args[2]
  2.0 89.2 %sinkhorn.1 = (f32[32,128]{1,0:T(8,128)}, f32[8,128]{1,0:T(8,128)}) custom-call(s32[32,8]{1,0:T(8,128)} %copy.9.cand, s32[32]{0:T(128)} %live.1, bf16[32,128,256]{2,1,0:T(8,128)(2,1)} %bitcast.7, bf16[8,128,256]{2,1,0:T(8,128)(2,1)} %bitcast.8, f32[32,128]{1,0:T(8,128)} %bitcast.9, f32[8,128]{1,0:T(8,128)} %bitcast.11, f32[8,128]{1,0:T(8,128)} %bitcast.12), custom_call_target="tpu_custom_call" | custom-call | tf_op jit(solution)/shard_map/sinkhorn/pallas_call | solution.py:483
  91.2 1.3 %copy.12 = f32[4096]{0:T(1024)} copy(f32[4096]{0:T(1024)} %bitcast.10) | data formatting | bytes 32768
  92.5 1.3 %copy.13 = f32[1024]{0:T(1024)} copy(f32[1024]{0:T(1024)} %bitcast.13) | data formatting | bytes 8192

commit v2 on v1

--- a/solution.py
+++ b/solution.py
@@ -34,6 +34,7 @@
     out_run,
     out_ref,
     ref_all,
+    own_v,
     run_v,
     tiles,
     v_all,
@@ -84,10 +85,26 @@
             barrier, inc=1, device_id=(lax.rem(g + k, GRP), n), device_id_type=MESH
         )
 
-    own_copy = pltpu.make_async_copy(ref_hbm, ref_all.at[pl.ds(n * 8, 8)], local_sem.at[0])
+    own_copy = pltpu.make_async_copy(ref_hbm, own_v, local_sem.at[0])
     own_copy.start()
     run_copy = pltpu.make_async_copy(run_hbm, run_v, local_sem.at[1])
     run_copy.start()
+
+    own_copy.wait()
+    for k in range(8):
+        ref_all[n * 8 + k] = own_v[k].T
+    lane64 = lax.broadcasted_iota(jnp.int32, (1, BLK), 1)
+
+    def table_step(b, carry):
+        for t in range(TOPC):
+            e = b * TOPC + t
+            onehot_t[pl.ds(e, 1)] = jnp.where(lane64 == cand[t, b], 1.0, 0.0).astype(F32)
+            rows_live[pl.ds(e, 1)] = jnp.where(
+                jnp.full((1, BLK), t, jnp.int32) < live[b], 1.0, 0.0
+            ).astype(F32)
+        return carry
+
+    lax.fori_loop(0, RB, table_step, 0)
 
     pl.semaphore_wait(barrier, NAR + GRP - 2)
 
@@ -131,7 +148,7 @@
     def region(block, half):
         if half is None:
             return ref_all.at[block]
-        return ref_all.at[block, pl.ds(half * 64, 64)]
+        return ref_all.at[block, pl.ds(half * 128, 128)]
 
     def gsend(block, half, ident, to, src=None):
         dst = region(block, half)
@@ -144,10 +161,15 @@
         send(dst, dst, pair_send.at[ident], pair_recv.at[ident], partner)
 
     own_a, own_b = n * 8 + x, n * 8 + 4 + z
-    gsend(own_a, None, 0, y_next, ref_hbm.at[x])
-    gsend(own_a, None, 1, y_prev, ref_hbm.at[x])
-    gsend(own_b, None, 2, y_next, ref_hbm.at[4 + z])
-    gsend(own_b, None, 3, y_prev, ref_hbm.at[4 + z])
+    gsend(own_a, None, 0, y_next, ref_all.at[own_a])
+    gsend(own_a, None, 1, y_prev, ref_all.at[own_a])
+    gsend(own_b, None, 2, y_next, ref_all.at[own_b])
+    gsend(own_b, None, 3, y_prev, ref_all.at[own_b])
+    y_over = (g, s_far)
+    x_over = (z * 4 + lax.rem(x + 2, 4), n)
+    z_over = (lax.rem(z + 2, 4) * 4 + x, n)
+    gsend(own_a, None, 4, y_over)
+    gsend(own_b, None, 5, y_over)
     for k in range(1, NAR):
         send(
             start,
@@ -156,41 +178,46 @@
             start_recv.at[k],
             (g, lax.rem(n + k, NAR)),
         )
-    send(ref_hbm, ref_all.at[pl.ds(n * 8, 8)], pair_send.at[30], pair_recv.at[30], partner)
+    own_part = ref_all.at[pl.ds(n * 8, 8)]
+    send(own_part, own_part, pair_send.at[30], pair_recv.at[30], partner)
     v_all[pl.ds(n * 8, 8)] = start[...]
 
-    lane64 = lax.broadcasted_iota(jnp.int32, (1, BLK), 1)
-
-    def table_step(b, carry):
-        for t in range(TOPC):
-            e = b * TOPC + t
-            onehot_t[pl.ds(e, 1)] = jnp.where(lane64 == cand[b, t], 1.0, 0.0).astype(F32)
-            rows_live[pl.ds(e, 1)] = jnp.where(
-                jnp.full((1, BLK), t, jnp.int32) < live[b], 1.0, 0.0
-            ).astype(F32)
-        return carry
-
-    lax.fori_loop(0, RB, table_step, 0)
+    eye = lax.broadcasted_iota(jnp.int32, (BLK, BLK), 0) == lax.broadcasted_iota(
+        jnp.int32, (BLK, BLK), 1
+    )
+    wide = (BLK, BLK)
+
+    def column(row):
+        spread = jnp.where(eye, jnp.broadcast_to(row, wide), 0.0)
+        return jnp.broadcast_to(jnp.sum(spread, axis=1, keepdims=True), wide)
+
+    def mass_step(b, carry):
+        row = run_mass[pl.ds(b, 1)]
+        a_col[b] = column(row)
+        loga_col[b] = column(jnp.log(row) * LOG2E)
+        return carry
+
+    lax.fori_loop(0, RB, mass_step, 0)
+    onehot[...] = onehot_t[...].T.astype(BF16)
 
     a_prev, a_next, a_far = s_prev * 8 + x, s_next * 8 + x, s_far * 8 + x
     b_prev, b_next, b_far = s_prev * 8 + 4 + z, s_next * 8 + 4 + z, s_far * 8 + 4 + z
 
-    def y_piece(block, ident, j, along_x, far_to, far_ident):
+    def y_piece(block, ident, j, along_x):
         arrived(region(block, None), gather_recv.at[ident])
-        if far_to is not None:
-            gsend(block, None, far_ident, far_to)
         base = 6 if along_x else 18
         up, down = (x_next, x_prev) if along_x else (z_next, z_prev)
         gsend(block, None, base + j, up)
         gsend(block, None, base + 3 + j, down)
+        gsend(block, None, base + 6 + j, x_over if along_x else z_over)
         to_partner(block, None, ident)
 
-    y_piece(a_prev, 0, 0, True, y_next, 4)
-    y_piece(b_next, 3, 1, False, y_prev, 5)
-    y_piece(a_next, 1, 1, True, None, None)
-    y_piece(b_prev, 2, 0, False, None, None)
-    y_piece(a_far, 4, 2, True, None, None)
-    y_piece(b_far, 5, 2, False, None, None)
+    y_piece(a_prev, 0, 0, True)
+    y_piece(b_next, 3, 1, False)
+    y_piece(a_next, 1, 1, True)
+    y_piece(b_prev, 2, 0, False)
+    y_piece(a_far, 4, 2, True)
+    y_piece(b_far, 5, 2, False)
 
     shard = (s_prev, s_next, s_far)
     x_up, x_down, x_far = lax.rem(x + 3, 4), lax.rem(x + 1, 4), lax.rem(x + 2, 4)
@@ -203,20 +230,16 @@
         from_next = shard[j] * 8 + off + (x_down if along_x else z_down)
         up, down = (x_next, x_prev) if along_x else (z_next, z_prev)
         arrived(region(from_prev, None), gather_recv.at[base + j])
-        gsend(from_prev, 0, base + 6 + j, up)
         to_partner(from_prev, None, base + j)
         arrived(region(from_next, None), gather_recv.at[base + 3 + j])
-        gsend(from_next, 1, base + 9 + j, down)
         to_partner(from_next, None, base + 3 + j)
 
     def far_piece(j, along_x):
         base = 6 if along_x else 18
         off = 0 if along_x else 4
         block = shard[j] * 8 + off + (x_far if along_x else z_far)
-        for half in range(2):
-            ident = base + 6 + 3 * half + j
-            arrived(region(block, half), gather_recv.at[ident])
-            to_partner(block, half, ident)
+        arrived(region(block, None), gather_recv.at[base + 6 + j])
+        to_partner(block, None, base + 6 + j)
 
     ring_piece(0, True)
     ring_piece(1, False)
@@ -225,24 +248,6 @@
     ring_piece(2, True)
     ring_piece(2, False)
 
-    eye = lax.broadcasted_iota(jnp.int32, (BLK, BLK), 0) == lax.broadcasted_iota(
-        jnp.int32, (BLK, BLK), 1
-    )
-    wide = (BLK, BLK)
-
-    def column(row):
-        spread = jnp.where(eye, jnp.broadcast_to(row, wide), 0.0)
-        return jnp.broadcast_to(jnp.sum(spread, axis=1, keepdims=True), wide)
-
-    def mass_step(b, carry):
-        row = run_mass[pl.ds(b, 1)]
-        a_col[b] = column(row)
-        loga_col[b] = column(jnp.log(row) * LOG2E)
-        return carry
-
-    lax.fori_loop(0, RB, mass_step, 0)
-    onehot[...] = onehot_t[...].T.astype(BF16)
-
     for k in range(1, NAR):
         owner = lax.rem(n + NAR - k, NAR)
         arrived(v_all.at[pl.ds(owner * 8, 8)], start_recv.at[k])
@@ -250,7 +255,7 @@
     def pick_rows(table, to):
         def step(b, carry):
             for t in range(TOPC):
-                to[pl.ds(b * TOPC + t, 1)] = table[pl.ds(cand[b, t], 1)]
+                to[pl.ds(b * TOPC + t, 1)] = table[pl.ds(cand[t, b], 1)]
             return carry
 
         lax.fori_loop(0, RB, step, 0)
@@ -269,8 +274,6 @@
     other = partner[1]
     arrived(ref_all.at[pl.ds(other * 8, 8)], pair_recv.at[30])
     o_shard = tuple(s + 1 - 2 * c for s in shard)
-    for j in range(3):
-        pass
     pieces = []
     pieces += [(o_shard[0] * 8 + x, None, 0), (o_shard[1] * 8 + x, None, 1)]
     pieces += [(o_shard[0] * 8 + 4 + z, None, 2), (o_shard[1] * 8 + 4 + z, None, 3)]
@@ -282,11 +285,9 @@
         ):
             pieces.append((o_shard[j] * 8 + off + up, None, base + j))
             pieces.append((o_shard[j] * 8 + off + down, None, base + 3 + j))
-            pieces.append((o_shard[j] * 8 + off + far, 0, base + 6 + j))
-            pieces.append((o_shard[j] * 8 + off + far, 1, base + 9 + j))
+            pieces.append((o_shard[j] * 8 + off + far, None, base + 6 + j))
     for block, half, ident in pieces:
         arrived(region(block, half), pair_recv.at[ident])
-    own_copy.wait()
     run_copy.wait()
 
     def cost_step(b, carry):
@@ -294,9 +295,9 @@
         top = None
         for h in range(TOPC // 2):
             e = b * TOPC + 2 * h
-            both = jnp.concatenate([ref_all[cand[b, 2 * h]], ref_all[cand[b, 2 * h + 1]]], axis=0)
+            both = jnp.concatenate([ref_all[cand[2 * h, b]], ref_all[cand[2 * h + 1, b]]], axis=1)
             prod = lax.dot_general(
-                run, both, (((1,), (1,)), ((), ())), preferred_element_type=F32
+                run, both, (((1,), (0,)), ((), ())), preferred_element_type=F32
             ) * (LOG2E / 8.0)
             for q in range(2):
                 s = prod[:, q * BLK : (q + 1) * BLK]
@@ -306,7 +307,7 @@
         r_col[b] = jnp.broadcast_to(jnp.max(top, axis=1, keepdims=True), wide)
         return carry
 
-    lax.fori_loop(0, RB, cost_step, 0, unroll=2)
+    lax.fori_loop(0, RB, cost_step, 0, unroll=4)
 
     def row_step(b, carry):
         top = r_col[b]
@@ -319,7 +320,7 @@
         u_col[b] = loga_col[b] - (top + jnp.log(total) * LOG2E)
         return carry
 
-    lax.fori_loop(0, RB, row_step, 0, unroll=2)
+    lax.fori_loop(0, RB, row_step, 0, unroll=4)
 
     def column_step(b, carry):
         u = u_col[b]
@@ -333,7 +334,7 @@
             rows_t[pl.ds(e, 1)] = jnp.sum(p, axis=0, keepdims=True)
         return carry
 
-    lax.fori_loop(0, RB, column_step, 0, unroll=2)
+    lax.fori_loop(0, RB, column_step, 0, unroll=4)
     alive = rows_live[...] > 0.5
     rows_m[...] = jnp.where(alive, rows_m[...], FLOOR)
     block_id = lax.broadcasted_iota(jnp.int32, (REFB, BLK), 0)
@@ -342,11 +343,11 @@
         for t in range(TOPC):
             e = b * TOPC + t
             top = jnp.maximum(
-                top, jnp.where(block_id == cand[b, t], rows_m[pl.ds(e, 1)], FLOOR)
+                top, jnp.where(block_id == cand[t, b], rows_m[pl.ds(e, 1)], FLOOR)
             )
         return top
 
-    top = lax.fori_loop(0, RB, peak_step, jnp.full((REFB, BLK), FLOOR, F32))
+    top = lax.fori_loop(0, RB, peak_step, jnp.full((REFB, BLK), FLOOR, F32), unroll=2)
     peak[...] = top
     pick_rows(peak, rows_a)
 
@@ -460,19 +461,24 @@
             rows_a[pl.ds(e, 1)] = jnp.sum(tiles[e] * alpha, axis=0, keepdims=True)
         return carry
 
-    lax.fori_loop(0, RB, second_rows, 0, unroll=2)
-    lax.fori_loop(0, RB, columns, 0, unroll=2)
+    lax.fori_loop(0, RB, second_rows, 0, unroll=4)
+    lax.fori_loop(0, RB, columns, 0, unroll=4)
     second = reduced(1, spread(rows_a[...] * rows_m[...]), plain_sum)
     gathered(1, ref_mass[...] / second)
     pick_rows(ag_buf.at[1], rows_a)
     rows_t[...] = rows_m[...] * rows_a[...]
-    lax.fori_loop(0, RB, third_rows, 0, unroll=2)
-    lax.fori_loop(0, RB, columns, 0, unroll=2)
+    lax.fori_loop(0, RB, third_rows, 0, unroll=4)
+    lax.fori_loop(0, RB, columns, 0, unroll=4)
     third = reduced(2, spread(rows_a[...] * rows_m[...]), plain_sum)
     out_ref[...] = (v_one + jnp.log(ref_mass[...] / third) * LOG2E) * (0.5 * LN2)
 
     for copy in sent:
         copy.wait_send()
+
+
+def write_out(run_in, ref_in, run_out, ref_out):
+    run_out[...] = run_in[...]
+    ref_out[...] = ref_in[...]
 
 
 def shards(run_desc, ref_desc, candidates, live_slots, run_mass, ref_mass, ref_start):
@@ -489,7 +495,8 @@
         in_specs=[smem, smem, hbm, hbm, vmem, vmem, vmem],
         out_specs=(vmem, vmem),
         scratch_shapes=[
-            pltpu.VMEM((REFB, BLK, D), BF16),
+            pltpu.VMEM((REFB, D, BLK), BF16),
+            pltpu.VMEM((8, BLK, D), BF16),
             pltpu.VMEM((RB, BLK, D), BF16),
             pltpu.VMEM((ENT, BLK, BLK), F32),
             pltpu.VMEM((REFB, BLK), F32),
@@ -530,7 +537,7 @@
         ),
         name="sinkhorn",
     )(
-        candidates,
+        candidates.T,
         live_slots,
         run_desc.reshape(RB, BLK, D),
         ref_desc.reshape(8, BLK, D),
@@ -538,6 +545,16 @@
         ref_mass.reshape(8, BLK),
         ref_start.reshape(8, BLK),
     )
+    run_potential, ref_potential = pl.pallas_call(
+        write_out,
+        out_shape=(
+            jax.ShapeDtypeStruct((RB, BLK), F32),
+            jax.ShapeDtypeStruct((8, BLK), F32),
+        ),
+        in_specs=[vmem, vmem],
+        out_specs=(vmem, vmem),
+        name="write_out",
+    )(run_potential, ref_potential)
     return run_potential.reshape(-1), ref_potential.reshape(-1)
 
 

time: 94.1 us -> 82.8 us (0.88)
  Pallas kernels: 89.2 us -> 82 us
  local copies, waits for them, and re-layouts: 3.95 us -> 0 us
    pallas_call x1, Pallas kernels: 89.2 us -> 80.6 us  [shards(): pl.pallas_call(kernel, out_shape=(jax.ShapeDtypeStruct((RB, BLK), F32), j...]
    unnamed x3 -> x0, local copies, waits for them, and re-layouts: 3.95 us -> none
    pallas_call x0 -> x1, Pallas kernels: none -> 1.33 us  [shards(): pl.pallas_call(write_out, out_shape=(jax.ShapeDtypeStruct((RB, BLK), F32)...]
where the time goes in v2:
time: 82.8 us; the launch traced here: 82.6 us
  Pallas kernels  82 us (99%)
    pallas_call x1, Pallas kernels, shards(): pl.pallas_call(kernel, out_shape=(jax.ShapeDtypeStruct((RB, BLK), F32), j...  80.6 us

profile of v2, /device:TPU:1, one launch (start us, length us, event | category | flops | bytes accessed | tf_op | source)
XLA Modules:
  0.0 82.6 jit_solution(9450683024415920472)
XLA Ops:
  0.6 80.6 %sinkhorn.1 = (f32[32,128]{1,0:T(8,128)}, f32[8,128]{1,0:T(8,128)}) custom-call(s32[8,32]{1,0:T(8,128)} %bitcast.11, s32[32]{0:T(128)} %live.1, bf16[32,128,256]{2,1,0:T(8,128)(2,1)} %bitcast.8, bf16[8,128,256]{2,1,0:T(8,128)(2,1)} %bitcast.9, f32[32,128]{1,0:T(8,128)} %bitcast.10, f32[8,128]{1,0:T(8,128)} %bitcast.12, f32[8,128]{1,0:T(8,128)} %bitcast.13), custom_call_target="tpu_custom_call" | custom-call | tf_op jit(solution)/shard_map/sinkhorn/pallas_call | solution.py:489
  81.3 1.3 %write_out.1 = (f32[32,128]{1,0:T(8,128)}, f32[8,128]{1,0:T(8,128)}) custom-call(f32[32,128]{1,0:T(8,128)} %get-tuple-element.6.run_in, f32[8,128]{1,0:T(8,128)} %get-tuple-element.7.ref_in), custom_call_target="tpu_custom_call" | custom-call | tf_op jit(solution)/shard_map/write_out/pallas_call | solution.py:548

commit v3 on v2

--- a/solution.py
+++ b/solution.py
@@ -37,6 +37,9 @@
     own_v,
     run_v,
     tiles,
+    raw,
+    tops,
+    us,
     v_all,
     rows_a,
     rows_m,
@@ -55,6 +58,7 @@
     ar_buf,
     final,
     ag_buf,
+    here_sem,
     local_sem,
     own_send,
     gather_send,
@@ -76,14 +80,19 @@
     y, c = lax.div(n, 2), lax.rem(n, 2)
 
     barrier = pltpu.get_barrier_semaphore()
-    for k in range(1, NAR):
-        pl.semaphore_signal(
-            barrier, inc=1, device_id=(g, lax.rem(n + k, NAR)), device_id_type=MESH
-        )
-    for k in range(1, GRP):
-        pl.semaphore_signal(
-            barrier, inc=1, device_id=(lax.rem(g + k, GRP), n), device_id_type=MESH
-        )
+    partner = (g, y * 2 + 1 - c)
+    y_next = (g, lax.rem(y + 1, 4) * 2 + c)
+    y_prev = (g, lax.rem(y + 3, 4) * 2 + c)
+    x_next = (z * 4 + lax.rem(x + 1, 4), n)
+    x_prev = (z * 4 + lax.rem(x + 3, 4), n)
+    z_next = (lax.rem(z + 1, 4) * 4 + x, n)
+    z_prev = (lax.rem(z + 3, 4) * 4 + x, n)
+    y_over = (g, lax.rem(y + 2, 4) * 2 + c)
+    x_over = (z * 4 + lax.rem(x + 2, 4), n)
+    z_over = (lax.rem(z + 2, 4) * 4 + x, n)
+    rings = (y_next, y_prev, y_over, x_next, x_prev, x_over, z_next, z_prev, z_over)
+    for to in (*rings, partner):
+        pl.semaphore_signal(barrier, inc=1, device_id=to, device_id_type=MESH)
 
     own_copy = pltpu.make_async_copy(ref_hbm, own_v, local_sem.at[0])
     own_copy.start()
@@ -106,15 +115,10 @@
 
     lax.fori_loop(0, RB, table_step, 0)
 
-    pl.semaphore_wait(barrier, NAR + GRP - 2)
-
-    partner = (g, y * 2 + 1 - c)
-    y_next = (g, lax.rem(y + 1, 4) * 2 + c)
-    y_prev = (g, lax.rem(y + 3, 4) * 2 + c)
-    x_next = (z * 4 + lax.rem(x + 1, 4), n)
-    x_prev = (z * 4 + lax.rem(x + 3, 4), n)
-    z_next = (lax.rem(z + 1, 4) * 4 + x, n)
-    z_prev = (lax.rem(z + 3, 4) * 4 + x, n)
+    pl.semaphore_wait(barrier, 10)
+    for to in (z_next, z_prev, z_over, partner):
+        pl.semaphore_signal(here_sem, inc=1, device_id=to, device_id_type=MESH)
+
     s_prev = y_prev[1]
     s_next = y_next[1]
     s_far = lax.rem(y + 2, 4) * 2 + c
@@ -165,11 +169,31 @@
     gsend(own_a, None, 1, y_prev, ref_all.at[own_a])
     gsend(own_b, None, 2, y_next, ref_all.at[own_b])
     gsend(own_b, None, 3, y_prev, ref_all.at[own_b])
-    y_over = (g, s_far)
-    x_over = (z * 4 + lax.rem(x + 2, 4), n)
-    z_over = (lax.rem(z + 2, 4) * 4 + x, n)
     gsend(own_a, None, 4, y_over)
     gsend(own_b, None, 5, y_over)
+    own_part = ref_all.at[pl.ds(n * 8, 8)]
+    send(own_part, own_part, pair_send.at[30], pair_recv.at[30], partner)
+    v_all[pl.ds(n * 8, 8)] = start[...]
+
+    eye = lax.broadcasted_iota(jnp.int32, (BLK, BLK), 0) == lax.broadcasted_iota(
+        jnp.int32, (BLK, BLK), 1
+    )
+    wide = (BLK, BLK)
+
+    def column(row):
+        spread = jnp.where(eye, jnp.broadcast_to(row, wide), 0.0)
+        return jnp.broadcast_to(jnp.sum(spread, axis=1, keepdims=True), wide)
+
+    def mass_step(b, carry):
+        row = run_mass[pl.ds(b, 1)]
+        a_col[b] = column(row)
+        loga_col[b] = column(jnp.log(row) * LOG2E)
+        return carry
+
+    lax.fori_loop(0, RB, mass_step, 0)
+    onehot[...] = onehot_t[...].T.astype(BF16)
+
+    pl.semaphore_wait(here_sem, 4)
     for k in range(1, NAR):
         send(
             start,
@@ -178,27 +202,6 @@
             start_recv.at[k],
             (g, lax.rem(n + k, NAR)),
         )
-    own_part = ref_all.at[pl.ds(n * 8, 8)]
-    send(own_part, own_part, pair_send.at[30], pair_recv.at[30], partner)
-    v_all[pl.ds(n * 8, 8)] = start[...]
-
-    eye = lax.broadcasted_iota(jnp.int32, (BLK, BLK), 0) == lax.broadcasted_iota(
-        jnp.int32, (BLK, BLK), 1
-    )
-    wide = (BLK, BLK)
-
-    def column(row):
-        spread = jnp.where(eye, jnp.broadcast_to(row, wide), 0.0)
-        return jnp.broadcast_to(jnp.sum(spread, axis=1, keepdims=True), wide)
-
-    def mass_step(b, carry):
-        row = run_mass[pl.ds(b, 1)]
-        a_col[b] = column(row)
-        loga_col[b] = column(jnp.log(row) * LOG2E)
-        return carry
-
-    lax.fori_loop(0, RB, mass_step, 0)
-    onehot[...] = onehot_t[...].T.astype(BF16)
 
     a_prev, a_next, a_far = s_prev * 8 + x, s_next * 8 + x, s_far * 8 + x
     b_prev, b_next, b_far = s_prev * 8 + 4 + z, s_next * 8 + 4 + z, s_far * 8 + 4 + z
@@ -290,51 +293,70 @@
         arrived(region(block, half), pair_recv.at[ident])
     run_copy.wait()
 
-    def cost_step(b, carry):
-        run = run_v[b]
-        top = None
-        for h in range(TOPC // 2):
-            e = b * TOPC + 2 * h
-            both = jnp.concatenate([ref_all[cand[2 * h, b]], ref_all[cand[2 * h + 1, b]]], axis=1)
-            prod = lax.dot_general(
-                run, both, (((1,), (0,)), ((), ())), preferred_element_type=F32
-            ) * (LOG2E / 8.0)
-            for q in range(2):
-                s = prod[:, q * BLK : (q + 1) * BLK]
-                tiles[e + q] = s
-                s = s + rows_a[pl.ds(e + q, 1)]
-                top = s if top is None else jnp.maximum(top, s)
-        r_col[b] = jnp.broadcast_to(jnp.max(top, axis=1, keepdims=True), wide)
-        return carry
-
-    lax.fori_loop(0, RB, cost_step, 0, unroll=4)
-
-    def row_step(b, carry):
-        top = r_col[b]
-        total = None
-        for t in range(TOPC):
+    def cost_part(b, slot, h, top):
+        both = jnp.concatenate([ref_all[cand[2 * h, b]], ref_all[cand[2 * h + 1, b]]], axis=1)
+        prod = lax.dot_general(
+            run_v[b], both, (((1,), (0,)), ((), ())), preferred_element_type=F32
+        ) * (LOG2E / 8.0)
+        for q in range(2):
+            s = prod[:, q * BLK : (q + 1) * BLK]
+            raw[slot][2 * h + q] = s
+            s = s + rows_a[pl.ds(b * TOPC + 2 * h + q, 1)]
+            top = s if top is None else jnp.maximum(top, s)
+        return top
+
+    def cost_end(slot, top):
+        tops[slot][...] = jnp.broadcast_to(jnp.max(top, axis=1, keepdims=True), wide)
+
+    def row_part(b, slot, h, total):
+        for t in (2 * h, 2 * h + 1):
+            p = jnp.exp2(raw[slot][t] + rows_a[pl.ds(b * TOPC + t, 1)] - tops[slot][...])
+            total = p if total is None else total + p
+        return total
+
+    def row_end(b, slot, total):
+        total = jnp.broadcast_to(jnp.sum(total, axis=1, keepdims=True), wide)
+        u = loga_col[b] - (tops[slot][...] + jnp.log(total) * LOG2E)
+        u_col[b] = u
+        us[slot][...] = u
+
+    def column_part(b, slot, h):
+        for t in (2 * h, 2 * h + 1):
             e = b * TOPC + t
-            p = jnp.exp2(tiles[e] + rows_a[pl.ds(e, 1)] - top)
-            total = p if total is None else total + p
-        total = jnp.broadcast_to(jnp.sum(total, axis=1, keepdims=True), wide)
-        u_col[b] = loga_col[b] - (top + jnp.log(total) * LOG2E)
-        return carry
-
-    lax.fori_loop(0, RB, row_step, 0, unroll=4)
-
-    def column_step(b, carry):
-        u = u_col[b]
-        for t in range(TOPC):
-            e = b * TOPC + t
-            s = tiles[e] + u
+            s = raw[slot][t] + us[slot][...]
             m = jnp.max(s, axis=0, keepdims=True)
             p = jnp.exp2(s - m)
             tiles[e] = p
             rows_m[pl.ds(e, 1)] = m
             rows_t[pl.ds(e, 1)] = jnp.sum(p, axis=0, keepdims=True)
+
+    def stage(b, at, cost=True, row=True, col=True):
+        top = total = None
+        for h in range(TOPC // 2):
+            if col:
+                column_part(b - 2, (at + 2) % 4, h)
+            if row:
+                total = row_part(b - 1, (at + 3) % 4, h, total)
+            if cost:
+                top = cost_part(b, at, h, top)
+        if row:
+            row_end(b - 1, (at + 3) % 4, total)
+        if cost:
+            cost_end(at, top)
+
+    stage(0, 0, row=False, col=False)
+    stage(1, 1, col=False)
+
+    def first_step(k, carry):
+        for q in range(4):
+            stage(2 + 4 * k + q, (2 + q) % 4)
         return carry
 
-    lax.fori_loop(0, RB, column_step, 0, unroll=4)
+    lax.fori_loop(0, 28 // 4, first_step, 0)
+    stage(30, 2)
+    stage(31, 3)
+    stage(32, 0, cost=False)
+    stage(33, 1, cost=False, row=False)
     alive = rows_live[...] > 0.5
     rows_m[...] = jnp.where(alive, rows_m[...], FLOOR)
     block_id = lax.broadcasted_iota(jnp.int32, (REFB, BLK), 0)
@@ -384,7 +406,7 @@
             total = total + p
         return total
 
-    def reduced(it, value, join):
+    def reduced(it, value, join, meanwhile=None):
         dense[it] = value
         for k in range(1, NAR):
             to = lax.rem(n + k, NAR)
@@ -396,6 +418,8 @@
                 (g, to),
             )
         rs_buf[it, n] = dense[it, pl.ds(n * 8, 8)]
+        if meanwhile is not None:
+            meanwhile()
         for k in range(1, NAR):
             arrived(rs_buf.at[it, lax.rem(n + NAR - k, NAR)], rs_recv.at[it, k])
         mine = join([rs_buf[it, k] for k in range(NAR)])
@@ -443,14 +467,12 @@
             total = p if total is None else total + p
         return jnp.broadcast_to(jnp.sum(total, axis=1, keepdims=True), wide)
 
-    def second_rows(b, carry):
+    def scale_rows(b, carry):
         r_col[b] = a_col[b] / row_sums(b)
         return carry
 
-    def third_rows(b, carry):
-        alpha = a_col[b] / row_sums(b)
-        r_col[b] = alpha
-        u = (u_col[b] + jnp.log(alpha) * LOG2E) * (0.5 * LN2)
+    def run_output(b, carry):
+        u = (u_col[b] + jnp.log(r_col[b]) * LOG2E) * (0.5 * LN2)
         out_run[pl.ds(b, 1)] = jnp.sum(jnp.where(eye, u, 0.0), axis=0, keepdims=True)
         return carry
 
@@ -461,15 +483,20 @@
             rows_a[pl.ds(e, 1)] = jnp.sum(tiles[e] * alpha, axis=0, keepdims=True)
         return carry
 
-    lax.fori_loop(0, RB, second_rows, 0, unroll=4)
+    lax.fori_loop(0, RB, scale_rows, 0, unroll=4)
     lax.fori_loop(0, RB, columns, 0, unroll=4)
     second = reduced(1, spread(rows_a[...] * rows_m[...]), plain_sum)
     gathered(1, ref_mass[...] / second)
     pick_rows(ag_buf.at[1], rows_a)
     rows_t[...] = rows_m[...] * rows_a[...]
-    lax.fori_loop(0, RB, third_rows, 0, unroll=4)
+    lax.fori_loop(0, RB, scale_rows, 0, unroll=4)
     lax.fori_loop(0, RB, columns, 0, unroll=4)
-    third = reduced(2, spread(rows_a[...] * rows_m[...]), plain_sum)
+    third = reduced(
+        2,
+        spread(rows_a[...] * rows_m[...]),
+        plain_sum,
+        lambda: lax.fori_loop(0, RB, run_output, 0, unroll=2),
+    )
     out_ref[...] = (v_one + jnp.log(ref_mass[...] / third) * LOG2E) * (0.5 * LN2)
 
     for copy in sent:
@@ -499,6 +526,9 @@
             pltpu.VMEM((8, BLK, D), BF16),
             pltpu.VMEM((RB, BLK, D), BF16),
             pltpu.VMEM((ENT, BLK, BLK), F32),
+            [pltpu.VMEM((TOPC, BLK, BLK), F32)] * 4,
+            [pltpu.VMEM((BLK, BLK), F32)] * 4,
+            [pltpu.VMEM((BLK, BLK), F32)] * 4,
             pltpu.VMEM((REFB, BLK), F32),
             pltpu.VMEM((ENT, BLK), F32),
             pltpu.VMEM((ENT, BLK), F32),
@@ -517,6 +547,7 @@
             pltpu.VMEM((3, GRP, 8, BLK), F32),
             pltpu.VMEM((2, 8, BLK), F32),
             pltpu.VMEM((2, REFB, BLK), F32),
+            pltpu.SemaphoreType.REGULAR,
             dma((2,)),
             dma((1,)),
             dma((32,)),

time: 82.8 us -> 81 us (0.978)
  Pallas kernels: 82 us -> 80.1 us
    pallas_call x1, Pallas kernels: 80.6 us -> 78.7 us  [shards(): pl.pallas_call(kernel, out_shape=(jax.ShapeDtypeStruct((RB, BLK), F32), j...]
where the time goes in v3:
time: 81 us; the launch traced here: 80.7 us
  Pallas kernels  80.1 us (99%)
    pallas_call x1, Pallas kernels, shards(): pl.pallas_call(kernel, out_shape=(jax.ShapeDtypeStruct((RB, BLK), F32), j...  78.7 us

profile of v3, /device:TPU:1, one launch (start us, length us, event | category | flops | bytes accessed | tf_op | source)
XLA Modules:
  0.0 80.7 jit_solution(12158148662716103844)
XLA Ops:
  0.6 78.7 %sinkhorn.1 = (f32[32,128]{1,0:T(8,128)}, f32[8,128]{1,0:T(8,128)}) custom-call(s32[8,32]{1,0:T(8,128)} %bitcast.11, s32[32]{0:T(128)} %live.1, bf16[32,128,256]{2,1,0:T(8,128)(2,1)} %bitcast.8, bf16[8,128,256]{2,1,0:T(8,128)(2,1)} %bitcast.9, f32[32,128]{1,0:T(8,128)} %bitcast.10, f32[8,128]{1,0:T(8,128)} %bitcast.12, f32[8,128]{1,0:T(8,128)} %bitcast.13), custom_call_target="tpu_custom_call" | custom-call | tf_op jit(solution)/shard_map/sinkhorn/pallas_call | solution.py:516
  79.4 1.3 %write_out.1 = (f32[32,128]{1,0:T(8,128)}, f32[8,128]{1,0:T(8,128)}) custom-call(f32[32,128]{1,0:T(8,128)} %get-tuple-element.6.run_in, f32[8,128]{1,0:T(8,128)} %get-tuple-element.7.ref_in), custom_call_target="tpu_custom_call" | custom-call | tf_op jit(solution)/shard_map/write_out/pallas_call | solution.py:579

commit v4 on v3

--- a/solution.py
+++ b/solution.py
@@ -24,15 +24,20 @@
 
 
 def kernel(
+    cand_in,
+    live_in,
+    run_hbm,
+    ref_hbm,
+    run_mass_in,
+    ref_mass_in,
+    start_in,
+    out_run,
+    out_ref,
     cand,
     live,
-    run_hbm,
-    ref_hbm,
     run_mass,
     ref_mass,
     start,
-    out_run,
-    out_ref,
     ref_all,
     own_v,
     run_v,
@@ -96,9 +101,25 @@
 
     own_copy = pltpu.make_async_copy(ref_hbm, own_v, local_sem.at[0])
     own_copy.start()
+    small = [
+        pltpu.make_async_copy(src, dst, local_sem.at[2 + k])
+        for k, (src, dst) in enumerate(
+            (
+                (cand_in, cand),
+                (live_in, live),
+                (start_in, start),
+                (run_mass_in, run_mass),
+                (ref_mass_in, ref_mass),
+            )
+        )
+    ]
+    for copy in small:
+        copy.start()
     run_copy = pltpu.make_async_copy(run_hbm, run_v, local_sem.at[1])
     run_copy.start()
 
+    for copy in small:
+        copy.wait()
     own_copy.wait()
     for k in range(8):
         ref_all[n * 8 + k] = own_v[k].T
@@ -113,7 +134,7 @@
             ).astype(F32)
         return carry
 
-    lax.fori_loop(0, RB, table_step, 0)
+    lax.fori_loop(0, RB, table_step, 0, unroll=2)
 
     pl.semaphore_wait(barrier, 10)
     for to in (z_next, z_prev, z_over, partner):
@@ -251,28 +272,28 @@
     ring_piece(2, True)
     ring_piece(2, False)
 
-    for k in range(1, NAR):
-        owner = lax.rem(n + NAR - k, NAR)
-        arrived(v_all.at[pl.ds(owner * 8, 8)], start_recv.at[k])
-
-    def pick_rows(table, to):
-        def step(b, carry):
-            for t in range(TOPC):
-                to[pl.ds(b * TOPC + t, 1)] = table[pl.ds(cand[t, b], 1)]
-            return carry
-
-        lax.fori_loop(0, RB, step, 0)
-
-    pick_rows(v_all, rows_a)
-    alive = rows_live[...] > 0.5
-    rows_a[...] = jnp.where(alive, rows_a[...] * (2.0 * LOG2E), FLOOR)
-
     far_piece(0, True)
     far_piece(1, False)
     far_piece(1, True)
     far_piece(0, False)
     far_piece(2, True)
     far_piece(2, False)
+
+    for k in range(1, NAR):
+        owner = lax.rem(n + NAR - k, NAR)
+        arrived(v_all.at[pl.ds(owner * 8, 8)], start_recv.at[k])
+
+    def pick_rows(table, to):
+        def step(b, carry):
+            for t in range(TOPC):
+                to[pl.ds(b * TOPC + t, 1)] = table[pl.ds(cand[t, b], 1)]
+            return carry
+
+        lax.fori_loop(0, RB, step, 0, unroll=4)
+
+    pick_rows(v_all, rows_a)
+    alive = rows_live[...] > 0.5
+    rows_a[...] = jnp.where(alive, rows_a[...] * (2.0 * LOG2E), FLOOR)
 
     other = partner[1]
     arrived(ref_all.at[pl.ds(other * 8, 8)], pair_recv.at[30])
@@ -510,7 +531,6 @@
 
 def shards(run_desc, ref_desc, candidates, live_slots, run_mass, ref_mass, ref_start):
     vmem = pl.BlockSpec(memory_space=pltpu.VMEM)
-    smem = pl.BlockSpec(memory_space=pltpu.SMEM)
     hbm = pl.BlockSpec(memory_space=pl.ANY)
     dma = pltpu.SemaphoreType.DMA
     run_potential, ref_potential = pl.pallas_call(
@@ -519,9 +539,14 @@
             jax.ShapeDtypeStruct((RB, BLK), F32),
             jax.ShapeDtypeStruct((8, BLK), F32),
         ),
-        in_specs=[smem, smem, hbm, hbm, vmem, vmem, vmem],
+        in_specs=[hbm] * 7,
         out_specs=(vmem, vmem),
         scratch_shapes=[
+            pltpu.SMEM((TOPC, RB), jnp.int32),
+            pltpu.SMEM((RB,), jnp.int32),
+            pltpu.VMEM((RB, BLK), F32),
+            pltpu.VMEM((8, BLK), F32),
+            pltpu.VMEM((8, BLK), F32),
             pltpu.VMEM((REFB, D, BLK), BF16),
             pltpu.VMEM((8, BLK, D), BF16),
             pltpu.VMEM((RB, BLK, D), BF16),
@@ -548,7 +573,7 @@
             pltpu.VMEM((2, 8, BLK), F32),
             pltpu.VMEM((2, REFB, BLK), F32),
             pltpu.SemaphoreType.REGULAR,
-            dma((2,)),
+            dma((7,)),
             dma((1,)),
             dma((32,)),
             dma((30,)),

time: 81 us -> 79.8 us (0.985)
  Pallas kernels: 80.1 us -> 79 us
    pallas_call x1, Pallas kernels: 78.7 us -> 77.6 us  [shards(): pl.pallas_call(kernel, out_shape=(jax.ShapeDtypeStruct((RB, BLK), F32), j...]
where the time goes in v4:
time: 79.8 us; the launch traced here: 79.6 us
  Pallas kernels  79 us (99%)
    pallas_call x1, Pallas kernels, shards(): pl.pallas_call(kernel, out_shape=(jax.ShapeDtypeStruct((RB, BLK), F32), j...  77.6 us

profile of v4, /device:TPU:1, one launch (start us, length us, event | category | flops | bytes accessed | tf_op | source)
XLA Modules:
  0.0 79.6 jit_solution(6767519699414077010)
XLA Ops:
  0.6 77.6 %sinkhorn.1 = (f32[32,128]{1,0:T(8,128)}, f32[8,128]{1,0:T(8,128)}) custom-call(s32[8,32]{1,0:T(8,128)} %bitcast.11, s32[32]{0:T(128)} %live_in.1, bf16[32,128,256]{2,1,0:T(8,128)(2,1)} %bitcast.8, bf16[8,128,256]{2,1,0:T(8,128)(2,1)} %bitcast.9, f32[32,128]{1,0:T(8,128)} %bitcast.10, f32[8,128]{1,0:T(8,128)} %bitcast.12, f32[8,128]{1,0:T(8,128)} %bitcast.13), custom_call_target="tpu_custom_call" | custom-call | tf_op jit(solution)/shard_map/sinkhorn/pallas_call | solution.py:536
  78.3 1.3 %write_out.1 = (f32[32,128]{1,0:T(8,128)}, f32[8,128]{1,0:T(8,128)}) custom-call(f32[32,128]{1,0:T(8,128)} %get-tuple-element.6.run_in, f32[8,128]{1,0:T(8,128)} %get-tuple-element.7.ref_in), custom_call_target="tpu_custom_call" | custom-call | tf_op jit(solution)/shard_map/write_out/pallas_call | solution.py:604

commit v5 on v4

--- a/solution.py
+++ b/solution.py
@@ -158,6 +158,10 @@
         copy.start()
         sent.append(copy)
 
+    def drain(keep):
+        while len(sent) > keep:
+            sent.pop(0).wait_send()
+
     def arrived(dst, recv_sem):
         pltpu.make_async_remote_copy(
             src_ref=dst,
@@ -439,6 +443,7 @@
                 (g, to),
             )
         rs_buf[it, n] = dense[it, pl.ds(n * 8, 8)]
+        drain(NAR - 1)
         if meanwhile is not None:
             meanwhile()
         for k in range(1, NAR):
@@ -454,6 +459,7 @@
                 (lax.rem(g + k, GRP), n),
             )
         ar_buf[it, g] = mine
+        drain(GRP - 1)
         for k in range(1, GRP):
             arrived(ar_buf.at[it, lax.rem(g + GRP - k, GRP)], ar_recv.at[it, k])
         return join([ar_buf[it, k] for k in range(GRP)])
@@ -469,6 +475,7 @@
                 (g, lax.rem(n + k, NAR)),
             )
         ag_buf[it, pl.ds(n * 8, 8)] = value
+        drain(NAR - 1)
         for k in range(1, NAR):
             owner = lax.rem(n + NAR - k, NAR)
             arrived(ag_buf.at[it, pl.ds(owner * 8, 8)], ag_recv.at[it, k])
@@ -488,30 +495,42 @@
             total = p if total is None else total + p
         return jnp.broadcast_to(jnp.sum(total, axis=1, keepdims=True), wide)
 
-    def scale_rows(b, carry):
-        r_col[b] = a_col[b] / row_sums(b)
-        return carry
+    def scale_rows(b, slot):
+        alpha = a_col[b] / row_sums(b)
+        r_col[b] = alpha
+        tops[slot][...] = alpha
 
     def run_output(b, carry):
         u = (u_col[b] + jnp.log(r_col[b]) * LOG2E) * (0.5 * LN2)
         out_run[pl.ds(b, 1)] = jnp.sum(jnp.where(eye, u, 0.0), axis=0, keepdims=True)
         return carry
 
-    def columns(b, carry):
-        alpha = r_col[b]
+    def columns(b, slot):
+        alpha = tops[slot][...]
         for t in range(TOPC):
             e = b * TOPC + t
             rows_a[pl.ds(e, 1)] = jnp.sum(tiles[e] * alpha, axis=0, keepdims=True)
-        return carry
-
-    lax.fori_loop(0, RB, scale_rows, 0, unroll=4)
-    lax.fori_loop(0, RB, columns, 0, unroll=4)
+
+    def both_sides():
+        def step(k, carry):
+            for q in range(4):
+                scale_rows(1 + 4 * k + q, (1 + q) % 4)
+                columns(4 * k + q, q)
+            return carry
+
+        scale_rows(0, 0)
+        lax.fori_loop(0, 7, step, 0)
+        for b in range(28, 31):
+            scale_rows(b + 1, (b + 1) % 4)
+            columns(b, b % 4)
+        columns(31, 3)
+
+    both_sides()
     second = reduced(1, spread(rows_a[...] * rows_m[...]), plain_sum)
     gathered(1, ref_mass[...] / second)
     pick_rows(ag_buf.at[1], rows_a)
     rows_t[...] = rows_m[...] * rows_a[...]
-    lax.fori_loop(0, RB, scale_rows, 0, unroll=4)
-    lax.fori_loop(0, RB, columns, 0, unroll=4)
+    both_sides()
     third = reduced(
         2,
         spread(rows_a[...] * rows_m[...]),
@@ -520,8 +539,7 @@
     )
     out_ref[...] = (v_one + jnp.log(ref_mass[...] / third) * LOG2E) * (0.5 * LN2)
 
-    for copy in sent:
-        copy.wait_send()
+    drain(0)
 
 
 def write_out(run_in, ref_in, run_out, ref_out):

time: 79.8 us -> 78.9 us (0.989)
  Pallas kernels: 79 us -> 78 us
    pallas_call x1, Pallas kernels: 77.6 us -> 76.7 us  [shards(): pl.pallas_call(kernel, out_shape=(jax.ShapeDtypeStruct((RB, BLK), F32), j...]
where the time goes in v5:
time: 78.9 us; the launch traced here: 78.7 us
  Pallas kernels  78 us (99%)
    pallas_call x1, Pallas kernels, shards(): pl.pallas_call(kernel, out_shape=(jax.ShapeDtypeStruct((RB, BLK), F32), j...  76.7 us

profile of v5, /device:TPU:1, one launch (start us, length us, event | category | flops | bytes accessed | tf_op | source)
XLA Modules:
  0.0 78.7 jit_solution(4110133262696571815)
XLA Ops:
  0.6 76.7 %sinkhorn.1 = (f32[32,128]{1,0:T(8,128)}, f32[8,128]{1,0:T(8,128)}) custom-call(s32[8,32]{1,0:T(8,128)} %bitcast.11, s32[32]{0:T(128)} %live_in.1, bf16[32,128,256]{2,1,0:T(8,128)(2,1)} %bitcast.8, bf16[8,128,256]{2,1,0:T(8,128)(2,1)} %bitcast.9, f32[32,128]{1,0:T(8,128)} %bitcast.10, f32[8,128]{1,0:T(8,128)} %bitcast.12, f32[8,128]{1,0:T(8,128)} %bitcast.13), custom_call_target="tpu_custom_call" | custom-call | tf_op jit(solution)/shard_map/sinkhorn/pallas_call | solution.py:554
  77.3 1.3 %write_out.1 = (f32[32,128]{1,0:T(8,128)}, f32[8,128]{1,0:T(8,128)}) custom-call(f32[32,128]{1,0:T(8,128)} %get-tuple-element.6.run_in, f32[8,128]{1,0:T(8,128)} %get-tuple-element.7.ref_in), custom_call_target="tpu_custom_call" | custom-call | tf_op jit(solution)/shard_map/write_out/pallas_call | solution.py:622

commit v6 on v5

--- a/solution.py
+++ b/solution.py
@@ -450,7 +450,7 @@
             arrived(rs_buf.at[it, lax.rem(n + NAR - k, NAR)], rs_recv.at[it, k])
         mine = join([rs_buf[it, k] for k in range(NAR)])
         part[it] = mine
-        for k in range(1, GRP):
+        for k in (10, 6, 9, 11, 5, 7, 8, 2, 14, 13, 1, 3, 15, 4, 12):
             send(
                 part.at[it],
                 ar_buf.at[it, g],

time: 78.9 us -> 78.6 us (level)
  no operation moved by 1% of the time
where the time goes in v6:
time: 78.6 us; the launch traced here: 78.4 us
  Pallas kernels  77.8 us (99%)
    pallas_call x1, Pallas kernels, shards(): pl.pallas_call(kernel, out_shape=(jax.ShapeDtypeStruct((RB, BLK), F32), j...  76.5 us

profile of v6, /device:TPU:1, one launch (start us, length us, event | category | flops | bytes accessed | tf_op | source)
XLA Modules:
  0.0 78.4 jit_solution(8530865594345564161)
XLA Ops:
  0.6 76.5 %sinkhorn.1 = (f32[32,128]{1,0:T(8,128)}, f32[8,128]{1,0:T(8,128)}) custom-call(s32[8,32]{1,0:T(8,128)} %bitcast.11, s32[32]{0:T(128)} %live_in.1, bf16[32,128,256]{2,1,0:T(8,128)(2,1)} %bitcast.8, bf16[8,128,256]{2,1,0:T(8,128)(2,1)} %bitcast.9, f32[32,128]{1,0:T(8,128)} %bitcast.10, f32[8,128]{1,0:T(8,128)} %bitcast.12, f32[8,128]{1,0:T(8,128)} %bitcast.13), custom_call_target="tpu_custom_call" | custom-call | tf_op jit(solution)/shard_map/sinkhorn/pallas_call | solution.py:554
  77.1 1.3 %write_out.1 = (f32[32,128]{1,0:T(8,128)}, f32[8,128]{1,0:T(8,128)}) custom-call(f32[32,128]{1,0:T(8,128)} %get-tuple-element.6.run_in, f32[8,128]{1,0:T(8,128)} %get-tuple-element.7.ref_in), custom_call_target="tpu_custom_call" | custom-call | tf_op jit(solution)/shard_map/write_out/pallas_call | solution.py:622
